TPU v7x, 768 devices: a whole 4x8x12 slice. The times are simulated.
768 devices in a mesh: ctx: 16 (over z_hi, x), fsdp: 48 (over z_lo, y, core).
Axes of the slice: x: 4, y: 8, z: 12 (z_hi: 4, z_lo: 3; z = z_hi * 3 + z_lo), core: 2. Of those that a mesh axis runs over, the one named last changes fastest.
Arguments:
- queries: bfloat16 [98304, 2048], P(('ctx', 'fsdp')), may hold values from -8 to 8
- keys: bfloat16 [98304, 1024], P(('ctx', 'fsdp')), may hold values from -8 to 8
- values: bfloat16 [98304, 1024], P(('ctx', 'fsdp')), may hold values from -6 to 6
- grad_out: bfloat16 [98304, 2048], P(('ctx', 'fsdp')), may hold values from -6 to 6
- segment: int32 [98304], P(('ctx', 'fsdp')), may hold values from 0 to 191, never falling along the last dimension, each value on 1 to 2048 neighbouring positions
Outputs:
- grad_queries: bfloat16 [98304, 2048], P(('ctx', 'fsdp'))
- grad_keys: bfloat16 [98304, 1024], P(('ctx', 'fsdp'))
- grad_values: bfloat16 [98304, 1024], P(('ctx', 'fsdp'))
Inputs may be any that keep to these rules, and one draw needn't show every extreme that they name: `segment`: document ids never fall along the sequence; every document holds 1 to 2048 tokens and one holds exactly 2048.
All inputs are finite; a program needn't handle non-finite values.
Results may differ from a plain program's by a relative error of at most 0.0071.
Values may be sent and summed in bfloat16 or wider, within the bound.
A program may use at most 32 MiB of HBM per device.

v0:
```python
import jax
import jax.numpy as jnp
from jax import lax
from jax.sharding import PartitionSpec as P

HEAD_DIM = 128
WINDOW = 512


softcap = 50.0
inv_scale = 1.0 / 12.0


def from_behind(shard, axis, by):
    devices = lax.axis_size(axis)
    pairs = [(i, i + by) for i in range(devices) if 0 <= i + by < devices]
    return lax.ppermute(shard, axis, pairs)


def tile_grads(query_rows, key_rows, value_rows, grad_rows, visible):
    raw_scores = jnp.einsum(
        "ngrd,mgd->grnm", query_rows, key_rows, preferred_element_type=jnp.float32
    )
    capped = softcap * jnp.tanh(raw_scores * inv_scale / softcap)
    weights = jnp.where(visible[None, None], jnp.exp(capped), jnp.float32(0.0))
    totals = jnp.sum(weights, axis=-1, keepdims=True)
    probs = weights / totals
    probs_low = probs.astype(jnp.bfloat16)
    attended = jnp.einsum(
        "grnm,mgd->ngrd", probs_low, value_rows, preferred_element_type=jnp.float32
    )
    row_terms = jnp.transpose(
        jnp.sum(grad_rows.astype(jnp.float32) * attended, axis=-1), (1, 2, 0)
    )[..., None]
    dprobs = jnp.einsum("ngrd,mgd->grnm", grad_rows, value_rows, preferred_element_type=jnp.float32)
    dscore = probs * (dprobs - row_terms) * (1.0 - (capped / softcap) ** 2) * inv_scale
    dscore_low = dscore.astype(jnp.bfloat16)
    grad_q = jnp.einsum("grnm,mgd->ngrd", dscore_low, key_rows, preferred_element_type=jnp.float32)
    grad_k = jnp.einsum(
        "grnm,ngrd->mgd", dscore_low, query_rows, preferred_element_type=jnp.float32
    )
    grad_v = jnp.einsum("grnm,ngrd->mgd", probs_low, grad_rows, preferred_element_type=jnp.float32)
    return (grad_q, grad_k, grad_v)


def group_grads(query_rows, key_rows, value_rows, grad_rows, visible):
    kv_heads = query_rows.shape[1]
    group_step = 2
    step_count = kv_heads // group_step

    def split_heads(array):
        shaped = array.reshape((array.shape[0], step_count, group_step) + array.shape[2:])
        return jnp.moveaxis(shaped, 1, 0)

    def join_heads(array):
        joined = jnp.moveaxis(array, 0, 1)
        return joined.reshape((joined.shape[0], kv_heads) + joined.shape[3:])

    def per_step(pieces):
        return tile_grads(pieces[0], pieces[1], pieces[2], pieces[3], visible)

    grad_q, grad_k, grad_v = lax.map(
        per_step,
        (
            split_heads(query_rows),
            split_heads(key_rows),
            split_heads(value_rows),
            split_heads(grad_rows),
        ),
    )
    return (join_heads(grad_q), join_heads(grad_k), join_heads(grad_v))


def local(queries, keys, values, grad_out, segment):
    tok_rows = queries.shape[0]
    kv_width = keys.shape[1]
    kv_heads = kv_width // HEAD_DIM
    group_size = queries.shape[1] // kv_width
    reach = (WINDOW + tok_rows - 1) // tok_rows
    block_rows = (reach + 1) * tok_rows
    earlier = []
    for distance in range(1, reach + 1):
        earlier.append(from_behind((keys, values, segment), ("ctx", "fsdp"), distance))
    ordered = earlier[::-1] + [(keys, values, segment)]
    key_block = jnp.concatenate([member[0] for member in ordered], 0)
    value_block = jnp.concatenate([member[1] for member in ordered], 0)
    seg_block = jnp.concatenate([member[2] for member in ordered], 0)
    device_index = lax.axis_index(("ctx", "fsdp"))
    first_row = device_index * tok_rows
    query_pos = first_row + jnp.arange(tok_rows, dtype=jnp.int32)
    key_pos = first_row - reach * tok_rows + jnp.arange(block_rows, dtype=jnp.int32)
    offsets = query_pos[:, None] - key_pos[None, :]
    visible = (
        (segment[:, None] == seg_block[None, :])
        & (offsets >= 0)
        & (offsets < WINDOW)
        & (key_pos[None, :] >= 0)
    )
    query_rows = queries.reshape(tok_rows, kv_heads, group_size, HEAD_DIM)
    grad_rows = grad_out.reshape(tok_rows, kv_heads, group_size, HEAD_DIM)
    key_rows = key_block.reshape(block_rows, kv_heads, HEAD_DIM)
    value_rows = value_block.reshape(block_rows, kv_heads, HEAD_DIM)
    grad_q, grad_k, grad_v = group_grads(query_rows, key_rows, value_rows, grad_rows, visible)
    grad_k = grad_k.reshape(block_rows, kv_width)
    grad_v = grad_v.reshape(block_rows, kv_width)

    def piece_of(array, distance):
        return array[(reach - distance) * tok_rows : (reach - distance + 1) * tok_rows]

    total_k = piece_of(grad_k, 0)
    total_v = piece_of(grad_v, 0)
    for distance in range(1, reach + 1):
        arrived = from_behind(
            (piece_of(grad_k, distance), piece_of(grad_v, distance)), ("ctx", "fsdp"), -distance
        )
        total_k = total_k + arrived[0]
        total_v = total_v + arrived[1]
    grad_queries = grad_q.reshape(tok_rows, queries.shape[1]).astype(jnp.bfloat16)
    return (grad_queries, total_k.astype(jnp.bfloat16), total_v.astype(jnp.bfloat16))


def solution(mesh):
    return jax.shard_map(
        local,
        mesh=mesh,
        in_specs=(
            P(("ctx", "fsdp"), None),
            P(("ctx", "fsdp"), None),
            P(("ctx", "fsdp"), None),
            P(("ctx", "fsdp"), None),
            P(("ctx", "fsdp")),
        ),
        out_specs=(P(("ctx", "fsdp"), None), P(("ctx", "fsdp"), None), P(("ctx", "fsdp"), None)),
        check_vma=False,
    )
```

profile of v0, /device:TPU:207, one launch (start us, length us, event | category | flops | bytes accessed | tf_op | source)
XLA Modules:
  0.0 255.8 jit_solution(6939442072529458374)
XLA Ops:
  0.7 3.3 %collective-permute-start.6 = (s32[128]{0:T(128)}, s32[128]{0:T(128)S(1)}, u32[]{:S(2)}, u32[]{:S(2)}) collective-permute-start(s32[128]{0:T(128)} %param.11), channel_id=1, source_target_pairs={{0,2},{1,3},{2,4},{3,5},{4,6},{5,7},{6,8},{7,9},{8,10},{9,11},{10,... | collective-permute-start | bytes 1544 | tf_op jit(solution)/shard_map/ppermute | solution.py:17
  4.0 6.3 %collective-permute-start.5 = (s32[128]{0:T(128)}, s32[128]{0:T(128)S(1)}, u32[]{:S(2)}, u32[]{:S(2)}) collective-permute-start(s32[128]{0:T(128)} %param.11), channel_id=1, source_target_pairs={{0,3},{1,4},{2,5},{3,6},{4,7},{5,8},{6,9},{7,10},{8,11},{9,12},{10... | collective-permute-start | bytes 1544 | tf_op jit(solution)/shard_map/ppermute | solution.py:17
  10.3 2.4 collective-permute-start.4
  12.7 2.1 collective-permute-start.7
  15.9 2.5 collective-permute-start.11
  21.0 4.4 %collective-permute-start.10 = (bf16[128,1024]{0,1:T(8,128)(2,1)S(1)}, bf16[128,1024]{0,1:T(8,128)(2,1)S(1)}, u32[]{:S(2)}, u32[]{:S(2)}) collective-permute-start(bf16[128,1024]{0,1:T(8,128)(2,1)S(1)} %copy.43), channel_id=1, source_target_pairs={{0,2},{1,3},{2,4},{3,5},{4,6},{5,7},{6,8},{7,9},{8,10},{9,11},{10,... | collective-permute-start | bytes 786440 | tf_op jit(solution)/shard_map/ppermute | solution.py:17
  25.4 3.2 %collective-permute-start.2 = (bf16[128,1024]{0,1:T(8,128)(2,1)S(1)}, bf16[128,1024]{0,1:T(8,128)(2,1)S(1)}, u32[]{:S(2)}, u32[]{:S(2)}) collective-permute-start(bf16[128,1024]{0,1:T(8,128)(2,1)S(1)} %copy.37), channel_id=1, source_target_pairs={{0,2},{1,3},{2,4},{3,5},{4,6},{5,7},{6,8},{7,9},{8,10},{9,11},{10,... | collective-permute-start | bytes 786440 | tf_op jit(solution)/shard_map/ppermute | solution.py:17
  28.7 4.2 %collective-permute-start = (bf16[128,1024]{0,1:T(8,128)(2,1)S(1)}, bf16[128,1024]{0,1:T(8,128)(2,1)S(1)}, u32[]{:S(2)}, u32[]{:S(2)}) collective-permute-start(bf16[128,1024]{0,1:T(8,128)(2,1)S(1)} %copy.37), channel_id=1, source_target_pairs={{0,4},{1,5},{2,6},{3,7},{4,8},{5,9},{6,10},{7,11},{8,12},{9,13},{1... | collective-permute-start | bytes 786440 | tf_op jit(solution)/shard_map/ppermute | solution.py:17
  32.9 5.0 %collective-permute-start.1 = (bf16[128,1024]{0,1:T(8,128)(2,1)S(1)}, bf16[128,1024]{0,1:T(8,128)(2,1)S(1)}, u32[]{:S(2)}, u32[]{:S(2)}) collective-permute-start(bf16[128,1024]{0,1:T(8,128)(2,1)S(1)} %copy.37), channel_id=1, source_target_pairs={{0,3},{1,4},{2,5},{3,6},{4,7},{5,8},{6,9},{7,10},{8,11},{9,12},{10... | collective-permute-start | bytes 786440 | tf_op jit(solution)/shard_map/ppermute | solution.py:17
  38.0 18.3 %collective-permute-done = bf16[128,1024]{0,1:T(8,128)(2,1)S(1)} collective-permute-done((bf16[128,1024]{0,1:T(8,128)(2,1)S(1)}, bf16[128,1024]{0,1:T(8,128)(2,1)S(1)}, u32[]{:S(2)}, u32[]{:S(2)}) %collective-permute-start) | collective-permute-done | bytes 262176 | tf_op jit(solution)/shard_map/ppermute | solution.py:17
  58.2 2.1 collective-permute-start.9
  60.4 6.6 %collective-permute-start.8 = (bf16[128,1024]{0,1:T(8,128)(2,1)S(1)}, bf16[128,1024]{0,1:T(8,128)(2,1)S(1)}, u32[]{:S(2)}, u32[]{:S(2)}) collective-permute-start(bf16[128,1024]{0,1:T(8,128)(2,1)S(1)} %copy.43), channel_id=1, source_target_pairs={{0,4},{1,5},{2,6},{3,7},{4,8},{5,9},{6,10},{7,11},{8,12},{9,13},{1... | collective-permute-start | bytes 786440 | tf_op jit(solution)/shard_map/ppermute | solution.py:17
  67.2 22.2 %collective-permute-done.8 = bf16[128,1024]{0,1:T(8,128)(2,1)S(1)} collective-permute-done((bf16[128,1024]{0,1:T(8,128)(2,1)S(1)}, bf16[128,1024]{0,1:T(8,128)(2,1)S(1)}, u32[]{:S(2)}, u32[]{:S(2)}) %collective-permute-start.8) | collective-permute-done | bytes 262176 | tf_op jit(solution)/shard_map/ppermute | solution.py:17
  90.7 30.3 %while.17 = (s32[]{:T(128)}, bf16[4,128,2,2,128]{1,4,3,2,0:T(8,128)(2,1)}, f32[4,640,2,128]{1,3,2,0:T(8,128)}, f32[4,640,2,128]{1,3,2,0:T(8,128)}, bf16[4,640,2,...) while((s32[]{:T(128)}, ...), condition=%wide.region_3.4_spmd.clone, body=%wide.region_0.3_spmd.clone.sunk | while | flops 509983744 | bytes 16471885 | solution.py:62
  94.8 2.2 fusion.78
  102.4 2.3 fusion.78
  110.0 2.3 fusion.78
  117.5 2.3 fusion.78
  121.0 2.9 %fusion.38 = (f32[128,4,2,128]{0,3,2,1:T(8,128)}, f32[128,4,2,128]{0,3,2,1:T(8,128)}, f32[128,4,2,128]{0,3,2,1:T(8,128)S(1)}, f32[128,4,2,128]{0,3,2,1:T(8,128)}, f32[128,4,2,128]{0,3,2,1:T(8,128)S(1)}) fusion(f32[640,4,2,128]{0,3,2,1:T(8,128)} %bitcast.183), kind=kLoop, calls=%fused_computation.67 | loop fusion | bytes 5242880 | tf_op jit(solution)/shard_map/slice | solution.py:108
  124.9 2.2 copy.85
  129.0 2.0 collective-permute-start.18
  131.0 2.0 copy.87
  133.1 2.5 collective-permute-start.19
  135.6 2.1 copy.84
  137.6 2.1 collective-permute-start.16
  144.9 2.3 collective-permute-start.13
  148.8 8.3 %collective-permute-start.14 = (f32[128,1024]{1,0:T(8,128)}, f32[128,1024]{1,0:T(8,128)}, u32[]{:S(2)}, u32[]{:S(2)}) collective-permute-start(f32[128,1024]{1,0:T(8,128)} %copy.81), channel_id=1, source_target_pairs={{3,0},{4,1},{5,2},{6,3},{7,4},{8,5},{9,6},{10,7},{11,8},{12,9},{13... | collective-permute-start | bytes 1572872 | tf_op jit(solution)/shard_map/ppermute | solution.py:17
  157.1 39.5 %collective-permute-done.18 = f32[128,1024]{1,0:T(8,128)} collective-permute-done((f32[128,1024]{1,0:T(8,128)}, f32[128,1024]{1,0:T(8,128)}, u32[]{:S(2)}, u32[]{:S(2)}) %collective-permute-start.18) | collective-permute-done | bytes 524320 | tf_op jit(solution)/shard_map/ppermute | solution.py:17
  201.9 19.0 %collective-permute-done.16 = f32[128,1024]{1,0:T(8,128)} collective-permute-done((f32[128,1024]{1,0:T(8,128)}, f32[128,1024]{1,0:T(8,128)}, u32[]{:S(2)}, u32[]{:S(2)}) %collective-permute-start.16) | collective-permute-done | bytes 524320 | tf_op jit(solution)/shard_map/ppermute | solution.py:17
  220.9 2.4 add_convert_fusion
  224.7 28.6 %collective-permute-done.12 = f32[128,1024]{1,0:T(8,128)} collective-permute-done((f32[128,1024]{1,0:T(8,128)S(1)}, f32[128,1024]{1,0:T(8,128)}, u32[]{:S(2)}, u32[]{:S(2)}) %collective-permute-start.12) | collective-permute-done | bytes 524320 | tf_op jit(solution)/shard_map/ppermute | solution.py:17
  253.4 2.4 add_convert_fusion.1
  (124 shorter events, 44.4 us)
Async XLA Ops:
  0.6 19.1 %copy-start.5 = (bf16[128,2048]{1,0:T(8,128)(2,1)S(1)}, bf16[128,2048]{1,0:T(8,128)(2,1)}, u32[]{:S(2)}) copy-start(bf16[128,2048]{1,0:T(8,128)(2,1)} %param.7) | copy-start | bytes 1572868
  0.6 20.1 %copy-start.6 = (bf16[128,2048]{1,0:T(8,128)(2,1)S(1)}, bf16[128,2048]{1,0:T(8,128)(2,1)}, u32[]{:S(2)}) copy-start(bf16[128,2048]{1,0:T(8,128)(2,1)} %param.10) | copy-start | bytes 1572868
  0.7 28.0 %collective-permute-start.6 = (s32[128]{0:T(128)}, s32[128]{0:T(128)S(1)}, u32[]{:S(2)}, u32[]{:S(2)}) collective-permute-start(s32[128]{0:T(128)} %param.11), channel_id=1, source_target_pairs={{0,2},{1,3},{2,4},{3,5},{4,6},{5,7},{6,8},{7,9},{8,10},{9,11},{10,... | collective-permute-start | bytes 1544 | tf_op jit(solution)/shard_map/ppermute | solution.py:17
  4.0 21.4 %collective-permute-start.5 = (s32[128]{0:T(128)}, s32[128]{0:T(128)S(1)}, u32[]{:S(2)}, u32[]{:S(2)}) collective-permute-start(s32[128]{0:T(128)} %param.11), channel_id=1, source_target_pairs={{0,3},{1,4},{2,5},{3,6},{4,7},{5,8},{6,9},{7,10},{8,11},{9,12},{10... | collective-permute-start | bytes 1544 | tf_op jit(solution)/shard_map/ppermute | solution.py:17
  10.3 10.7 %collective-permute-start.4 = (s32[128]{0:T(128)}, s32[128]{0:T(128)S(1)}, u32[]{:S(2)}, u32[]{:S(2)}) collective-permute-start(s32[128]{0:T(128)} %param.11), channel_id=1, source_target_pairs={{0,4},{1,5},{2,6},{3,7},{4,8},{5,9},{6,10},{7,11},{8,12},{9,13},{1... | collective-permute-start | bytes 1544 | tf_op jit(solution)/shard_map/ppermute | solution.py:17
  12.7 20.2 %collective-permute-start.7 = (s32[128]{0:T(128)}, s32[128]{0:T(128)S(1)}, u32[]{:S(2)}, u32[]{:S(2)}) collective-permute-start(s32[128]{0:T(128)} %param.11), channel_id=1, source_target_pairs={{0,1},{1,2},{2,3},{3,4},{4,5},{5,6},{6,7},{7,8},{8,9},{9,10},{10,1... | collective-permute-start | bytes 1544 | tf_op jit(solution)/shard_map/ppermute | solution.py:17
  15.9 73.7 %collective-permute-start.11 = (bf16[128,1024]{0,1:T(8,128)(2,1)S(1)}, bf16[128,1024]{0,1:T(8,128)(2,1)}, u32[]{:S(2)}, u32[]{:S(2)}) collective-permute-start(bf16[128,1024]{0,1:T(8,128)(2,1)S(1)} %copy.43), channel_id=1, source_target_pairs={{0,1},{1,2},{2,3},{3,4},{4,5},{5,6},{6,7},{7,8},{8,9},{9,10},{10,1... | collective-permute-start | bytes 786440 | tf_op jit(solution)/shard_map/ppermute | solution.py:17
  18.5 19.4 %copy-start.10 = (s32[128]{0:T(128)S(1)}, s32[128]{0:T(128)}, u32[]{:S(2)}) copy-start(s32[128]{0:T(128)} %param.11) | copy-start | bytes 1540
  21.0 68.5 %collective-permute-start.10 = (bf16[128,1024]{0,1:T(8,128)(2,1)S(1)}, bf16[128,1024]{0,1:T(8,128)(2,1)S(1)}, u32[]{:S(2)}, u32[]{:S(2)}) collective-permute-start(bf16[128,1024]{0,1:T(8,128)(2,1)S(1)} %copy.43), channel_id=1, source_target_pairs={{0,2},{1,3},{2,4},{3,5},{4,6},{5,7},{6,8},{7,9},{8,10},{9,11},{10,... | collective-permute-start | bytes 786440 | tf_op jit(solution)/shard_map/ppermute | solution.py:17
  25.4 35.0 %collective-permute-start.2 = (bf16[128,1024]{0,1:T(8,128)(2,1)S(1)}, bf16[128,1024]{0,1:T(8,128)(2,1)S(1)}, u32[]{:S(2)}, u32[]{:S(2)}) collective-permute-start(bf16[128,1024]{0,1:T(8,128)(2,1)S(1)} %copy.37), channel_id=1, source_target_pairs={{0,2},{1,3},{2,4},{3,5},{4,6},{5,7},{6,8},{7,9},{8,10},{9,11},{10,... | collective-permute-start | bytes 786440 | tf_op jit(solution)/shard_map/ppermute | solution.py:17
  28.7 27.5 %collective-permute-start = (bf16[128,1024]{0,1:T(8,128)(2,1)S(1)}, bf16[128,1024]{0,1:T(8,128)(2,1)S(1)}, u32[]{:S(2)}, u32[]{:S(2)}) collective-permute-start(bf16[128,1024]{0,1:T(8,128)(2,1)S(1)} %copy.37), channel_id=1, source_target_pairs={{0,4},{1,5},{2,6},{3,7},{4,8},{5,9},{6,10},{7,11},{8,12},{9,13},{1... | collective-permute-start | bytes 786440 | tf_op jit(solution)/shard_map/ppermute | solution.py:17
  32.9 25.3 %collective-permute-start.1 = (bf16[128,1024]{0,1:T(8,128)(2,1)S(1)}, bf16[128,1024]{0,1:T(8,128)(2,1)S(1)}, u32[]{:S(2)}, u32[]{:S(2)}) collective-permute-start(bf16[128,1024]{0,1:T(8,128)(2,1)S(1)} %copy.37), channel_id=1, source_target_pairs={{0,3},{1,4},{2,5},{3,6},{4,7},{5,8},{6,9},{7,10},{8,11},{9,12},{10... | collective-permute-start | bytes 786440 | tf_op jit(solution)/shard_map/ppermute | solution.py:17
  56.2 10.9 %collective-permute-start.3 = (bf16[128,1024]{0,1:T(8,128)(2,1)S(1)}, bf16[128,1024]{0,1:T(8,128)(2,1)S(1)}, u32[]{:S(2)}, u32[]{:S(2)}) collective-permute-start(bf16[128,1024]{0,1:T(8,128)(2,1)S(1)} %copy.37), channel_id=1, source_target_pairs={{0,1},{1,2},{2,3},{3,4},{4,5},{5,6},{6,7},{7,8},{8,9},{9,10},{10,1... | collective-permute-start | bytes 786440 | tf_op jit(solution)/shard_map/ppermute | solution.py:17
  58.2 31.2 %collective-permute-start.9 = (bf16[128,1024]{0,1:T(8,128)(2,1)S(1)}, bf16[128,1024]{0,1:T(8,128)(2,1)S(1)}, u32[]{:S(2)}, u32[]{:S(2)}) collective-permute-start(bf16[128,1024]{0,1:T(8,128)(2,1)S(1)} %copy.43), channel_id=1, source_target_pairs={{0,3},{1,4},{2,5},{3,6},{4,7},{5,8},{6,9},{7,10},{8,11},{9,12},{10... | collective-permute-start | bytes 786440 | tf_op jit(solution)/shard_map/ppermute | solution.py:17
  60.4 29.0 %collective-permute-start.8 = (bf16[128,1024]{0,1:T(8,128)(2,1)S(1)}, bf16[128,1024]{0,1:T(8,128)(2,1)S(1)}, u32[]{:S(2)}, u32[]{:S(2)}) collective-permute-start(bf16[128,1024]{0,1:T(8,128)(2,1)S(1)} %copy.43), channel_id=1, source_target_pairs={{0,4},{1,5},{2,6},{3,7},{4,8},{5,9},{6,10},{7,11},{8,12},{9,13},{1... | collective-permute-start | bytes 786440 | tf_op jit(solution)/shard_map/ppermute | solution.py:17
  94.8 3.4 %copy-start.8 = (bf16[4,128,2,2,128]{1,4,3,2,0:T(8,128)(2,1)}, bf16[4,128,2,2,128]{1,4,3,2,0:T(8,128)(2,1)S(1)}, u32[]{:S(2)}) copy-start(bf16[4,128,2,2,128]{1,4,3,2,0:T(8,128)(2,1)S(1)} %fusion.77) | copy-start | bytes 1572868 | tf_op jit(solution)/shard_map/while
  102.4 3.5 %copy-start.8 = (bf16[4,128,2,2,128]{1,4,3,2,0:T(8,128)(2,1)}, bf16[4,128,2,2,128]{1,4,3,2,0:T(8,128)(2,1)S(1)}, u32[]{:S(2)}) copy-start(bf16[4,128,2,2,128]{1,4,3,2,0:T(8,128)(2,1)S(1)} %fusion.77) | copy-start | bytes 1572868 | tf_op jit(solution)/shard_map/while
  109.9 3.5 %copy-start.8 = (bf16[4,128,2,2,128]{1,4,3,2,0:T(8,128)(2,1)}, bf16[4,128,2,2,128]{1,4,3,2,0:T(8,128)(2,1)S(1)}, u32[]{:S(2)}) copy-start(bf16[4,128,2,2,128]{1,4,3,2,0:T(8,128)(2,1)S(1)} %fusion.77) | copy-start | bytes 1572868 | tf_op jit(solution)/shard_map/while
  117.5 3.5 %copy-start.8 = (bf16[4,128,2,2,128]{1,4,3,2,0:T(8,128)(2,1)}, bf16[4,128,2,2,128]{1,4,3,2,0:T(8,128)(2,1)S(1)}, u32[]{:S(2)}) copy-start(bf16[4,128,2,2,128]{1,4,3,2,0:T(8,128)(2,1)S(1)} %fusion.77) | copy-start | bytes 1572868 | tf_op jit(solution)/shard_map/while
  124.9 14.8 %copy-start = (f32[4,640,2,128]{1,3,2,0:T(8,128)S(1)}, f32[4,640,2,128]{1,3,2,0:T(8,128)}, u32[]{:S(2)}) copy-start(f32[4,640,2,128]{1,3,2,0:T(8,128)} %get-tuple-element.120) | copy-start | bytes 7864324
  127.1 21.7 %collective-permute-start.17 = (f32[128,1024]{1,0:T(8,128)}, f32[128,1024]{1,0:T(8,128)}, u32[]{:S(2)}, u32[]{:S(2)}) collective-permute-start(f32[128,1024]{1,0:T(8,128)} %copy.85), channel_id=1, source_target_pairs={{2,0},{3,1},{4,2},{5,3},{6,4},{7,5},{8,6},{9,7},{10,8},{11,9},{12,... | collective-permute-start | bytes 1572872 | tf_op jit(solution)/shard_map/ppermute | solution.py:17
  129.0 67.6 %collective-permute-start.18 = (f32[128,1024]{1,0:T(8,128)}, f32[128,1024]{1,0:T(8,128)}, u32[]{:S(2)}, u32[]{:S(2)}) collective-permute-start(f32[128,1024]{1,0:T(8,128)} %copy.86), channel_id=1, source_target_pairs={{3,0},{4,1},{5,2},{6,3},{7,4},{8,5},{9,6},{10,7},{11,8},{12,9},{13... | collective-permute-start | bytes 1572872 | tf_op jit(solution)/shard_map/ppermute | solution.py:17
  133.1 65.5 %collective-permute-start.19 = (f32[128,1024]{1,0:T(8,128)}, f32[128,1024]{1,0:T(8,128)}, u32[]{:S(2)}, u32[]{:S(2)}) collective-permute-start(f32[128,1024]{1,0:T(8,128)} %copy.87), channel_id=1, source_target_pairs={{4,0},{5,1},{6,2},{7,3},{8,4},{9,5},{10,6},{11,7},{12,8},{13,9},{1... | collective-permute-start | bytes 1572872 | tf_op jit(solution)/shard_map/ppermute | solution.py:17
  137.6 83.3 %collective-permute-start.16 = (f32[128,1024]{1,0:T(8,128)}, f32[128,1024]{1,0:T(8,128)}, u32[]{:S(2)}, u32[]{:S(2)}) collective-permute-start(f32[128,1024]{1,0:T(8,128)} %copy.84), channel_id=1, source_target_pairs={{1,0},{2,1},{3,2},{4,3},{5,4},{6,5},{7,6},{8,7},{9,8},{10,9},{11,1... | collective-permute-start | bytes 1572872 | tf_op jit(solution)/shard_map/ppermute | solution.py:17
  141.3 1.3 copy-start.4
  141.3 1.6 copy-start.3
  142.8 57.7 %copy-start.9 = (bf16[4,128,2,2,128]{1,4,3,2,0:T(8,128)(2,1)S(1)}, bf16[4,128,2,2,128]{1,4,3,2,0:T(8,128)(2,1)}, u32[]{:S(2)}) copy-start(bf16[4,128,2,2,128]{1,4,3,2,0:T(8,128)(2,1)} %get-tuple-element.119) | copy-start | bytes 1572868
  144.9 56.8 %copy-start.1 = (f32[128,4,2,128]{0,3,2,1:T(8,128)S(1)}, f32[128,4,2,128]{0,3,2,1:T(8,128)}, u32[]{:S(2)}) copy-start(f32[128,4,2,128]{0,3,2,1:T(8,128)} %get-tuple-element.205) | copy-start | bytes 1572868
  144.9 78.4 %collective-permute-start.13 = (f32[128,1024]{1,0:T(8,128)}, f32[128,1024]{1,0:T(8,128)}, u32[]{:S(2)}, u32[]{:S(2)}) collective-permute-start(f32[128,1024]{1,0:T(8,128)} %copy.80), channel_id=1, source_target_pairs={{2,0},{3,1},{4,2},{5,3},{6,4},{7,5},{8,6},{9,7},{10,8},{11,9},{12,... | collective-permute-start | bytes 1572872 | tf_op jit(solution)/shard_map/ppermute | solution.py:17
  148.8 75.9 %collective-permute-start.14 = (f32[128,1024]{1,0:T(8,128)}, f32[128,1024]{1,0:T(8,128)}, u32[]{:S(2)}, u32[]{:S(2)}) collective-permute-start(f32[128,1024]{1,0:T(8,128)} %copy.81), channel_id=1, source_target_pairs={{3,0},{4,1},{5,2},{6,3},{7,4},{8,5},{9,6},{10,7},{11,8},{12,9},{13... | collective-permute-start | bytes 1572872 | tf_op jit(solution)/shard_map/ppermute | solution.py:17
  196.6 28.1 %collective-permute-start.15 = (f32[128,1024]{1,0:T(8,128)S(1)}, f32[128,1024]{1,0:T(8,128)}, u32[]{:S(2)}, u32[]{:S(2)}) collective-permute-start(f32[128,1024]{1,0:T(8,128)S(1)} %copy.82), channel_id=1, source_target_pairs={{4,0},{5,1},{6,2},{7,3},{8,4},{9,5},{10,6},{11,7},{12,8},{13,9},{1... | collective-permute-start | bytes 1572872 | tf_op jit(solution)/shard_map/ppermute | solution.py:17
  198.6 54.8 %collective-permute-start.12 = (f32[128,1024]{1,0:T(8,128)S(1)}, f32[128,1024]{1,0:T(8,128)}, u32[]{:S(2)}, u32[]{:S(2)}) collective-permute-start(f32[128,1024]{1,0:T(8,128)S(1)} %copy.79), channel_id=1, source_target_pairs={{1,0},{2,1},{3,2},{4,3},{5,4},{6,5},{7,6},{8,7},{9,8},{10,9},{11,1... | collective-permute-start | bytes 1572872 | tf_op jit(solution)/shard_map/ppermute | solution.py:17
  (5 other events, 5.4 us)
where the time goes:
time: 257 us; the launch traced here: 256 us
  waiting for transfers between devices  131 us (51%)
  starting transfers between devices  66.9 us (26%)
  matrix products  25.7 us (10%)
  local copies, waits for them, and re-layouts  23.8 us (9%)
  other arithmetic  7.22 us (3%)
    ppermute x20, waiting for transfers between devices, from_behind(): return lax.ppermute(shard, axis, pairs)  131 us
    ppermute x20, starting transfers between devices, from_behind(): return lax.ppermute(shard, axis, pairs)  66.9 us
    slice x12, local copies, waits for them, and re-layouts, piece_of(): array[(reach - distance) * tok_rows:(reach - distance + 1) * tok_rows]  15.7 us
    dot_general x4, matrix products, tile_grads(): jnp.einsum('grnm,ngrd->mgd', dscore_low, query_rows, preferred_element_ty...  9.06 us
    dot_general x4, matrix products, tile_grads(): jnp.einsum('ngrd,mgd->grnm', query_rows, key_rows, preferred_element_type...  5.97 us
  transfers between devices with their start and end apart: 20, of which 7 were waited for; matrix products, arithmetic and copies ran while one was open for 7% of the time, Pallas kernels for 0%

commit v1 on v0

v1 whole, which is shorter than its diff:
```python
import functools

import jax
import jax.numpy as jnp
from jax import lax
from jax.experimental import pallas as pl
from jax.experimental.pallas import tpu as pltpu
from jax.sharding import PartitionSpec as P

TOK = 128
DIM = 128
WINDOW = 512
KVH = 4
GROUP = 2
KVW = KVH * DIM
QW = KVW * GROUP
CHIP = 2 * TOK
REACH = WINDOW // TOK
ROWS = WINDOW + CHIP
SPAN = WINDOW + TOK
CAP = 50.0
SCALE = 1.0 / 12.0

NT = (((1,), (1,)), ((), ()))
NN = (((1,), (0,)), ((), ()))
TN = (((0,), (0,)), ((), ()))


def mm(lhs, rhs, dims):
    return lax.dot_general(lhs, rhs, dims, preferred_element_type=jnp.float32)


def kernel(
    chips,
    fsdp,
    q_hbm,
    k_hbm,
    v_hbm,
    do_hbm,
    seg_hbm,
    dq_hbm,
    dk_hbm,
    dv_hbm,
    kv,
    q,
    do,
    seg,
    mask,
    part,
    far_out,
    far_in,
    near_out,
    near_in,
    dq,
    dkv,
    own_send,
    own_recv,
    relay_send,
    relay_recv,
    swap_send,
    swap_recv,
    seg_send,
    seg_recv,
    seg_relay_send,
    seg_relay_recv,
    far_send,
    far_recv,
    near_send,
    near_recv,
    dq_send,
    dq_recv,
    dkv_send,
    dkv_recv,
):
    index = lax.axis_index("ctx") * fsdp + lax.axis_index("fsdp")
    chip = index // 2
    me = index % 2
    other = 1 - me

    def device(which_chip, core):
        at = which_chip * 2 + core
        return (at // fsdp, at % fsdp)

    ahead = (chip + 1) % chips
    behind = (chip + chips - 1) % chips
    partner = device(chip, other)

    def remote(src, dst, send, recv, to):
        return pltpu.make_async_remote_copy(
            src_ref=src,
            dst_ref=dst,
            send_sem=send,
            recv_sem=recv,
            device_id=to,
            device_id_type=pl.DeviceIdType.MESH,
        )

    def wait(ref, sem):
        pltpu.make_async_copy(ref, ref, sem).wait()

    def lanes(start, size):
        return pl.ds(pl.multiple_of(start, DIM), size)

    def rows(core, base=0):
        return pl.ds(pl.multiple_of(base + core * TOK, TOK), TOK)

    barrier = pltpu.get_barrier_semaphore()
    for to in (
        partner,
        device(ahead, 0),
        device(ahead, 1),
        device(behind, 0),
        device(behind, 1),
    ):
        pl.semaphore_signal(barrier, inc=1, device_id=to, device_id_type=pl.DeviceIdType.MESH)
    pl.semaphore_wait(barrier, 5)

    def send_own(j):
        for core in range(2):
            for which, src in ((0, k_hbm), (1, v_hbm)):
                remote(
                    src.at[:, lanes(core * KVW + j * DIM, DIM)],
                    kv.at[which, rows(me, CHIP), lanes(j * DIM, DIM)],
                    own_send.at[j],
                    own_recv.at[j],
                    device(ahead, core),
                ).start()

    def head_rows(start, j):
        return kv.at[:, start : start + CHIP, lanes(j * DIM, DIM)]

    def relay(j):
        wait(head_rows(CHIP, j), own_recv.at[j])
        remote(
            head_rows(CHIP, j),
            head_rows(0, j),
            relay_send.at[j],
            relay_recv.at[j],
            device(ahead, me),
        ).start()

    for core in range(2):
        remote(
            seg_hbm, seg.at[2 + me], seg_send, seg_recv, device(ahead, core)
        ).start()
    send_own(0)
    send_own(1)
    remote(seg_hbm, seg.at[REACH + me], seg_send, seg_recv, partner).start()
    pltpu.make_async_copy(seg_hbm, seg.at[REACH + me], seg_recv).start()
    swaps = (
        (k_hbm, kv.at[0, rows(me, WINDOW), :], KVW),
        (v_hbm, kv.at[1, rows(me, WINDOW), :], KVW),
        (q_hbm, q.at[rows(me), :], QW),
        (do_hbm, do.at[rows(me), :], QW),
    )
    for n, (src, dst, width) in enumerate(swaps):
        remote(
            src.at[:, lanes(other * width, width)],
            dst,
            swap_send.at[n],
            swap_recv.at[n],
            partner,
        ).start()
        pltpu.make_async_copy(
            src.at[:, lanes(me * width, width)], dst, swap_recv.at[n]
        ).start()

    wait(seg.at[2:6], seg_recv)
    remote(
        seg.at[2:4], seg.at[0:2], seg_relay_send, seg_relay_recv, device(ahead, me)
    ).start()
    for j in range(2):
        relay(j)
        send_own(j + 2)

    wait(seg.at[0:2], seg_relay_recv)
    key_at = lax.broadcasted_iota(jnp.int32, (TOK, TOK), 0)
    query_at = lax.broadcasted_iota(jnp.int32, (TOK, TOK), 1)
    for b in range(6):
        wide = jnp.broadcast_to(seg[b].astype(jnp.float32), (TOK, TOK))
        key_seg = wide.T
        real = jnp.where(2 * chip - REACH + b >= 0, 1.0, 0.0)
        for s in range(2):
            distance = REACH + s - b
            if distance < 0 or distance > REACH:
                continue
            query_seg = jnp.broadcast_to(seg[REACH + s].astype(jnp.float32), (TOK, TOK))
            seen = jnp.where(key_seg == query_seg, real, 0.0)
            if distance == 0:
                seen = jnp.where(query_at >= key_at, seen, 0.0)
            if distance == REACH:
                seen = jnp.where(query_at < key_at, seen, 0.0)
            at = (b - s) * TOK
            mask[s, at : at + TOK, :] = seen

    wait(kv.at[0, WINDOW:ROWS, :], swap_recv.at[0])
    wait(kv.at[1, WINDOW:ROWS, :], swap_recv.at[1])
    wait(q, swap_recv.at[2])
    wait(do, swap_recv.at[3])

    def unit(j, s):
        cols = lanes(j * DIM, DIM)
        keys = kv[0, s * TOK : s * TOK + SPAN, cols]
        vals = kv[1, s * TOK : s * TOK + SPAN, cols]

        def stacked(ref):
            return jnp.concatenate(
                [
                    ref[s * TOK : (s + 1) * TOK, lanes((j * GROUP + r) * DIM, DIM)]
                    for r in range(GROUP)
                ],
                axis=0,
            )

        queries = stacked(q)
        grads = stacked(do)
        seen = jnp.concatenate([mask[s]] * GROUP, axis=1)
        t = jnp.tanh(mm(keys, queries, NT) * (SCALE / CAP))
        weights = jnp.exp(CAP * t) * seen
        total = jnp.sum(weights, axis=0, keepdims=True)
        probs = weights * (1.0 / total)
        probs_low = probs.astype(jnp.bfloat16)
        dprobs = mm(vals, grads, NT)
        row_term = jnp.sum(probs_low.astype(jnp.float32) * dprobs, axis=0, keepdims=True)
        dscore = probs * (dprobs - row_term) * ((1.0 - t * t) * SCALE)
        dscore_low = dscore.astype(jnp.bfloat16)
        grad_k = mm(dscore_low, queries, NN)
        grad_v = mm(probs_low, grads, NN)
        grad_q = mm(keys, dscore_low, TN).T
        for r in range(GROUP):
            dq[s * TOK : (s + 1) * TOK, lanes((j * GROUP + r) * DIM, DIM)] = grad_q[
                r * TOK : (r + 1) * TOK
            ].astype(jnp.bfloat16)
        return grad_k, grad_v

    def far_copy(j):
        return remote(
            far_out.at[j], far_in.at[j], far_send.at[j], far_recv.at[j], device(behind, me)
        )

    def near_copy(j):
        return remote(
            near_out.at[j], near_in.at[j], near_send.at[j], near_recv.at[j], device(behind, me)
        )

    def pass_on(j):
        wait(far_in.at[j], far_recv.at[j])
        near_out[j] = (part[j, :, 0:CHIP, :] + far_in[j].astype(jnp.float32)).astype(jnp.bfloat16)
        near_copy(j).start()

    def swap_dq(j):
        width = GROUP * DIM
        into = lanes(me * QW + j * width, width)
        cols = lanes(j * width, width)
        remote(
            dq.at[rows(other), cols], dq_hbm.at[:, into], dq_send.at[j], dq_recv.at[j], partner
        ).start()
        pltpu.make_async_copy(dq.at[rows(me), cols], dq_hbm.at[:, into], dq_recv.at[j]).start()

    def finish(j):
        wait(near_in.at[j], near_recv.at[j])
        dkv[:, :, lanes(j * DIM, DIM)] = (
            part[j, :, CHIP:WINDOW, :] + near_in[j].astype(jnp.float32)
        ).astype(jnp.bfloat16)
        cols = lanes(j * DIM, DIM)
        into = lanes(me * KVW + j * DIM, DIM)
        for which, out in ((0, dk_hbm), (1, dv_hbm)):
            remote(
                dkv.at[which, rows(other), cols],
                out.at[:, into],
                dkv_send.at[which, j],
                dkv_recv.at[which, j],
                partner,
            ).start()
            pltpu.make_async_copy(
                dkv.at[which, rows(me), cols], out.at[:, into], dkv_recv.at[which, j]
            ).start()

    @pl.loop(0, KVH)
    def _(j):
        wait(head_rows(0, j), relay_recv.at[j])
        first = unit(j, 0)
        second = unit(j, 1)
        for which in range(2):
            low, high = first[which], second[which]
            far_out[j, which, 0:TOK, :] = low[0:TOK].astype(jnp.bfloat16)
            far_out[j, which, TOK:CHIP, :] = (low[TOK:CHIP] + high[0:TOK]).astype(jnp.bfloat16)
            part[j, which, 0 : WINDOW - TOK, :] = low[CHIP:SPAN] + high[TOK:WINDOW]
            part[j, which, WINDOW - TOK : WINDOW, :] = high[WINDOW:SPAN]
        far_copy(j).start()
        swap_dq(j)

        @pl.when(j < 2)
        def _():
            relay(j + 2)

        @pl.when(j >= 1)
        def _():
            pass_on(j - 1)

    pass_on(KVH - 1)

    @pl.loop(0, KVH)
    def _(j):
        finish(j)

    wait(seg.at[2:5], seg_send)
    wait(seg.at[2:4], seg_relay_send)
    for n, (_, dst, _) in enumerate(swaps):
        wait(dst, swap_send.at[n])

    @pl.loop(0, KVH)
    def _(j):
        width = GROUP * DIM
        wait(head_rows(CHIP, j), own_send.at[j])
        wait(head_rows(0, j), relay_send.at[j])
        wait(far_out.at[j], far_send.at[j])
        wait(near_out.at[j], near_send.at[j])
        wait(dq.at[0:TOK, lanes(j * width, width)], dq_send.at[j])
        wait(dq.at[:, lanes(j * width, width)], dq_recv.at[j])
        for which in range(2):
            wait(dkv.at[which, 0:TOK, lanes(j * DIM, DIM)], dkv_send.at[which, j])
            wait(dkv.at[which, :, lanes(j * DIM, DIM)], dkv_recv.at[which, j])


def local(chips, fsdp, queries, keys, values, grad_out, segment):
    low = jnp.bfloat16
    dma = pltpu.SemaphoreType.DMA
    anywhere = pl.BlockSpec(memory_space=pl.ANY)
    return pl.pallas_call(
        functools.partial(kernel, chips, fsdp),
        out_shape=(
            jax.ShapeDtypeStruct(queries.shape, low),
            jax.ShapeDtypeStruct(keys.shape, low),
            jax.ShapeDtypeStruct(values.shape, low),
        ),
        in_specs=[anywhere] * 5,
        out_specs=(anywhere,) * 3,
        scratch_shapes=[
            pltpu.VMEM((2, ROWS, KVW), low),
            pltpu.VMEM((CHIP, QW), low),
            pltpu.VMEM((CHIP, QW), low),
            pltpu.VMEM((6, 1, TOK), jnp.int32),
            pltpu.VMEM((2, SPAN, TOK), jnp.float32),
            pltpu.VMEM((KVH, 2, WINDOW, DIM), jnp.float32),
            pltpu.VMEM((KVH, 2, CHIP, DIM), low),
            pltpu.VMEM((KVH, 2, CHIP, DIM), low),
            pltpu.VMEM((KVH, 2, CHIP, DIM), low),
            pltpu.VMEM((KVH, 2, CHIP, DIM), low),
            pltpu.VMEM((CHIP, QW), low),
            pltpu.VMEM((2, CHIP, KVW), low),
            dma((KVH,)),
            dma((KVH,)),
            dma((KVH,)),
            dma((KVH,)),
            dma((4,)),
            dma((4,)),
            dma(()),
            dma(()),
            dma(()),
            dma(()),
            dma((KVH,)),
            dma((KVH,)),
            dma((KVH,)),
            dma((KVH,)),
            dma((KVH,)),
            dma((KVH,)),
            dma((2, KVH)),
            dma((2, KVH)),
        ],
        compiler_params=pltpu.CompilerParams(collective_id=0, has_side_effects=True),
        name="window_grads",
    )(queries, keys, values, grad_out, segment.reshape(1, TOK))


def solution(mesh):
    fsdp = mesh.shape["fsdp"]
    chips = mesh.shape["ctx"] * fsdp // 2
    split = P(("ctx", "fsdp"), None)
    return jax.shard_map(
        functools.partial(local, chips, fsdp),
        mesh=mesh,
        in_specs=(split, split, split, split, P(("ctx", "fsdp"))),
        out_specs=(split, split, split),
        check_vma=False,
    )
```

time: 257 us -> 65.7 us (0.26)
  the two profiles are of different devices: /device:TPU:207 before, /device:TPU:1 now
where the time goes in v1:
time: 65.7 us; the launch traced here: 65.5 us
  Pallas kernels  61.2 us (93%)
  local copies, waits for them, and re-layouts  3.67 us (6%)
    pallas_call x1, Pallas kernels, local(): pl.pallas_call(functools.partial(kernel, chips, fsdp), out_shape=(jax.Sha...  61.2 us
    unnamed x7, local copies, waits for them, and re-layouts  3.67 us

profile of v1, /device:TPU:1, one launch (start us, length us, event | category | flops | bytes accessed | tf_op | source)
XLA Modules:
  0.0 65.5 jit_solution(7774452297550515489)
XLA Ops:
  0.6 61.2 %window_grads.1 = (bf16[128,2048]{1,0:T(8,128)(2,1)}, bf16[128,1024]{1,0:T(8,128)(2,1)}, bf16[128,1024]{1,0:T(8,128)(2,1)}) custom-call(bf16[128,2048]{1,0:T(8,128)(2,1)} %q_hbm.1, bf16[128,1024]{1,0:T(8,128)(2,1)} %k_hbm.1, bf16[128,1024]{1,0:T(8,128)(2,1)} %v_hbm.1, bf16[128,2048]{1,0:T(8,128)(2,1)} %do_hbm.1, s32[1,128]{1,0:T(1,128)} %bitcast.1), custom_call_target="tpu_custom_call" | custom-call | tf_op jit(solution)/shard_map/window_grads/pallas_call | solution.py:330
  61.8 0.0 copy-start.1
  61.8 1.9 %copy.11 = bf16[128,2048]{1,0:T(8,128)(2,1)} copy(bf16[128,2048]{1,0:T(8,128)(2,1)} %get-tuple-element.6) | data formatting | bytes 1048576
  63.7 0.0 copy-done.1
  63.7 0.0 copy-start
  63.7 0.7 %copy.12 = bf16[128,1024]{1,0:T(8,128)(2,1)} copy(bf16[128,1024]{1,0:T(8,128)(2,1)S(1)} %copy-done.1) | data formatting | bytes 524288
  64.5 0.3 copy-done
  64.8 0.7 %copy.13 = bf16[128,1024]{1,0:T(8,128)(2,1)} copy(bf16[128,1024]{1,0:T(8,128)(2,1)S(1)} %copy-done) | data formatting | bytes 524288
Async XLA Ops:
  61.8 1.9 %copy-start.1 = (bf16[128,1024]{1,0:T(8,128)(2,1)S(1)}, bf16[128,1024]{1,0:T(8,128)(2,1)}, u32[]{:S(2)}) copy-start(bf16[128,1024]{1,0:T(8,128)(2,1)} %get-tuple-element.7) | copy-start | bytes 786436
  63.7 1.0 %copy-start = (bf16[128,1024]{1,0:T(8,128)(2,1)S(1)}, bf16[128,1024]{1,0:T(8,128)(2,1)}, u32[]{:S(2)}) copy-start(bf16[128,1024]{1,0:T(8,128)(2,1)} %get-tuple-element.8) | copy-start | bytes 786436

commit v2 on v1

--- a/solution.py
+++ b/solution.py
@@ -38,21 +38,20 @@
     v_hbm,
     do_hbm,
     seg_hbm,
-    dq_hbm,
-    dk_hbm,
-    dv_hbm,
+    dq_out,
+    near_in,
+    own_in,
     kv,
     q,
     do,
     seg,
     mask,
     part,
+    own_out,
     far_out,
     far_in,
     near_out,
-    near_in,
     dq,
-    dkv,
     own_send,
     own_recv,
     relay_send,
@@ -61,6 +60,8 @@
     swap_recv,
     seg_send,
     seg_recv,
+    seg_swap_send,
+    seg_swap_recv,
     seg_relay_send,
     seg_relay_recv,
     far_send,
@@ -69,8 +70,9 @@
     near_recv,
     dq_send,
     dq_recv,
-    dkv_send,
-    dkv_recv,
+    part_send,
+    part_recv,
+    ready,
 ):
     index = lax.axis_index("ctx") * fsdp + lax.axis_index("fsdp")
     chip = index // 2
@@ -104,16 +106,27 @@
     def rows(core, base=0):
         return pl.ds(pl.multiple_of(base + core * TOK, TOK), TOK)
 
+    has_ahead = chip < chips - 1
+    has_behind = chip > 0
+    has_far = chip > 1
+
+    def signal(sem, to):
+        pl.semaphore_signal(sem, inc=1, device_id=to, device_id_type=pl.DeviceIdType.MESH)
+
     barrier = pltpu.get_barrier_semaphore()
-    for to in (
-        partner,
-        device(ahead, 0),
-        device(ahead, 1),
-        device(behind, 0),
-        device(behind, 1),
-    ):
-        pl.semaphore_signal(barrier, inc=1, device_id=to, device_id_type=pl.DeviceIdType.MESH)
-    pl.semaphore_wait(barrier, 5)
+    signal(barrier, partner)
+
+    @pl.when(has_behind)
+    def _():
+        signal(barrier, device(behind, 0))
+        signal(barrier, device(behind, 1))
+
+    pl.semaphore_wait(barrier, 1 + 2 * jnp.where(has_ahead, 1, 0))
+
+    @pl.when(has_ahead)
+    def _():
+        signal(ready, device(ahead, 0))
+        signal(ready, device(ahead, 1))
 
     def send_own(j):
         for core in range(2):
@@ -130,23 +143,34 @@
         return kv.at[:, start : start + CHIP, lanes(j * DIM, DIM)]
 
     def relay(j):
-        wait(head_rows(CHIP, j), own_recv.at[j])
-        remote(
-            head_rows(CHIP, j),
-            head_rows(0, j),
-            relay_send.at[j],
-            relay_recv.at[j],
-            device(ahead, me),
-        ).start()
-
-    for core in range(2):
-        remote(
-            seg_hbm, seg.at[2 + me], seg_send, seg_recv, device(ahead, core)
-        ).start()
-    send_own(0)
-    send_own(1)
-    remote(seg_hbm, seg.at[REACH + me], seg_send, seg_recv, partner).start()
-    pltpu.make_async_copy(seg_hbm, seg.at[REACH + me], seg_recv).start()
+        @pl.when(has_behind)
+        def _():
+            wait(head_rows(CHIP, j), own_recv.at[j])
+
+        @pl.when(has_behind & has_ahead)
+        def _():
+            remote(
+                head_rows(CHIP, j),
+                head_rows(0, j),
+                relay_send.at[j],
+                relay_recv.at[j],
+                device(ahead, me),
+            ).start()
+
+    @pl.when(has_ahead)
+    def _():
+        for core in range(2):
+            remote(seg_hbm, seg.at[2 + me], seg_send, seg_recv, device(ahead, core)).start()
+        send_own(0)
+        send_own(1)
+
+    @pl.when(chip <= 1)
+    def _():
+        send_own(2)
+        send_own(3)
+
+    remote(seg_hbm, seg.at[REACH + me], seg_swap_send, seg_swap_recv, partner).start()
+    pltpu.make_async_copy(seg_hbm, seg.at[REACH + me], seg_swap_recv).start()
     swaps = (
         (k_hbm, kv.at[0, rows(me, WINDOW), :], KVW),
         (v_hbm, kv.at[1, rows(me, WINDOW), :], KVW),
@@ -165,15 +189,49 @@
             src.at[:, lanes(me * width, width)], dst, swap_recv.at[n]
         ).start()
 
-    wait(seg.at[2:6], seg_recv)
-    remote(
-        seg.at[2:4], seg.at[0:2], seg_relay_send, seg_relay_recv, device(ahead, me)
-    ).start()
-    for j in range(2):
-        relay(j)
-        send_own(j + 2)
-
-    wait(seg.at[0:2], seg_relay_recv)
+    @pl.when(chip <= 1)
+    def _():
+        kv[:, 0:CHIP, :] = jnp.zeros((2, CHIP, KVW), kv.dtype)
+        seg[0:2] = jnp.zeros((2, 1, TOK), seg.dtype)
+
+    @pl.when(chip == 0)
+    def _():
+        kv[:, CHIP:WINDOW, :] = jnp.zeros((2, CHIP, KVW), kv.dtype)
+        seg[2:4] = jnp.zeros((2, 1, TOK), seg.dtype)
+
+    @pl.when(chip == chips - 1)
+    def _():
+        far_in[...] = jnp.zeros(far_in.shape, far_in.dtype)
+        near_in[...] = jnp.zeros(near_in.shape, near_in.dtype)
+
+    @pl.when(has_behind)
+    def _():
+        wait(seg.at[2:4], seg_recv)
+
+    @pl.when(has_behind & has_ahead)
+    def _():
+        remote(
+            seg.at[2:4], seg.at[0:2], seg_relay_send, seg_relay_recv, device(ahead, me)
+        ).start()
+
+    relay(0)
+    relay(1)
+
+    @pl.when(has_ahead & has_far)
+    def _():
+        send_own(2)
+        send_own(3)
+
+    wait(seg.at[4:6], seg_swap_recv)
+
+    @pl.when(has_far)
+    def _():
+        wait(seg.at[0:2], seg_relay_recv)
+
+    @pl.when(has_behind)
+    def _():
+        pl.semaphore_wait(ready, 2)
+
     key_at = lax.broadcasted_iota(jnp.int32, (TOK, TOK), 0)
     query_at = lax.broadcasted_iota(jnp.int32, (TOK, TOK), 1)
     for b in range(6):
@@ -238,117 +296,167 @@
             far_out.at[j], far_in.at[j], far_send.at[j], far_recv.at[j], device(behind, me)
         )
 
-    def near_copy(j):
-        return remote(
-            near_out.at[j], near_in.at[j], near_send.at[j], near_recv.at[j], device(behind, me)
-        )
+    def send_near(j):
+        for core in range(2):
+            remote(
+                near_out.at[j, :, core * TOK : (core + 1) * TOK, :],
+                near_in.at[:, :, lanes(me * KVW + j * DIM, DIM)],
+                near_send.at[j],
+                near_recv.at[me * KVH + j],
+                device(behind, core),
+            ).start()
 
     def pass_on(j):
-        wait(far_in.at[j], far_recv.at[j])
-        near_out[j] = (part[j, :, 0:CHIP, :] + far_in[j].astype(jnp.float32)).astype(jnp.bfloat16)
-        near_copy(j).start()
-
-    def swap_dq(j):
+        @pl.when(has_behind)
+        def _():
+            @pl.when(has_ahead)
+            def _():
+                wait(far_in.at[j], far_recv.at[j])
+
+            near_out[j] = (part[j] + far_in[j].astype(jnp.float32)).astype(
+                jnp.bfloat16
+            )
+            send_near(j)
+
+    def swap(j):
         width = GROUP * DIM
         into = lanes(me * QW + j * width, width)
         cols = lanes(j * width, width)
         remote(
-            dq.at[rows(other), cols], dq_hbm.at[:, into], dq_send.at[j], dq_recv.at[j], partner
+            dq.at[rows(other), cols], dq_out.at[:, into], dq_send.at[j], dq_recv.at[j], partner
         ).start()
-        pltpu.make_async_copy(dq.at[rows(me), cols], dq_hbm.at[:, into], dq_recv.at[j]).start()
-
-    def finish(j):
-        wait(near_in.at[j], near_recv.at[j])
-        dkv[:, :, lanes(j * DIM, DIM)] = (
-            part[j, :, CHIP:WINDOW, :] + near_in[j].astype(jnp.float32)
-        ).astype(jnp.bfloat16)
-        cols = lanes(j * DIM, DIM)
+        pltpu.make_async_copy(dq.at[rows(me), cols], dq_out.at[:, into], dq_recv.at[j]).start()
         into = lanes(me * KVW + j * DIM, DIM)
-        for which, out in ((0, dk_hbm), (1, dv_hbm)):
-            remote(
-                dkv.at[which, rows(other), cols],
-                out.at[:, into],
-                dkv_send.at[which, j],
-                dkv_recv.at[which, j],
-                partner,
-            ).start()
-            pltpu.make_async_copy(
-                dkv.at[which, rows(me), cols], out.at[:, into], dkv_recv.at[which, j]
-            ).start()
+        remote(
+            own_out.at[j, :, rows(other), :],
+            own_in.at[:, :, into],
+            part_send.at[j],
+            part_recv.at[j],
+            partner,
+        ).start()
+        pltpu.make_async_copy(
+            own_out.at[j, :, rows(me), :], own_in.at[:, :, into], part_recv.at[j]
+        ).start()
 
     @pl.loop(0, KVH)
     def _(j):
-        wait(head_rows(0, j), relay_recv.at[j])
+        @pl.when(has_far)
+        def _():
+            wait(head_rows(0, j), relay_recv.at[j])
+
         first = unit(j, 0)
         second = unit(j, 1)
         for which in range(2):
             low, high = first[which], second[which]
             far_out[j, which, 0:TOK, :] = low[0:TOK].astype(jnp.bfloat16)
             far_out[j, which, TOK:CHIP, :] = (low[TOK:CHIP] + high[0:TOK]).astype(jnp.bfloat16)
-            part[j, which, 0 : WINDOW - TOK, :] = low[CHIP:SPAN] + high[TOK:WINDOW]
-            part[j, which, WINDOW - TOK : WINDOW, :] = high[WINDOW:SPAN]
-        far_copy(j).start()
-        swap_dq(j)
-
-        @pl.when(j < 2)
-        def _():
-            relay(j + 2)
-
-        @pl.when(j >= 1)
-        def _():
-            pass_on(j - 1)
-
-    pass_on(KVH - 1)
-
-    @pl.loop(0, KVH)
-    def _(j):
-        finish(j)
-
-    wait(seg.at[2:5], seg_send)
-    wait(seg.at[2:4], seg_relay_send)
+            part[j, which] = low[CHIP:WINDOW] + high[TOK : WINDOW - TOK]
+            own_out[j, which, 0:TOK, :] = low[WINDOW:SPAN] + high[WINDOW - TOK : WINDOW]
+            own_out[j, which, TOK:CHIP, :] = high[WINDOW:SPAN]
+
+        @pl.when(has_far)
+        def _():
+            far_copy(j).start()
+
+        swap(j)
+
+        @pl.when(j == 1)
+        def _():
+            for n in range(2):
+                relay(n + 2)
+                pass_on(n)
+
+        @pl.when(j == KVH - 1)
+        def _():
+            pass_on(KVH - 2)
+            pass_on(KVH - 1)
+
+    @pl.when(has_ahead)
+    def _():
+        wait(seg.at[2:4], seg_send)
+
+    @pl.when(has_behind & has_ahead)
+    def _():
+        wait(seg.at[2:4], seg_relay_send)
+
+    wait(seg.at[REACH], seg_swap_send)
     for n, (_, dst, _) in enumerate(swaps):
         wait(dst, swap_send.at[n])
 
     @pl.loop(0, KVH)
     def _(j):
         width = GROUP * DIM
-        wait(head_rows(CHIP, j), own_send.at[j])
-        wait(head_rows(0, j), relay_send.at[j])
-        wait(far_out.at[j], far_send.at[j])
-        wait(near_out.at[j], near_send.at[j])
+        @pl.when(has_ahead)
+        def _():
+            wait(head_rows(CHIP, j), own_send.at[j])
+
+        @pl.when(has_behind & has_ahead)
+        def _():
+            wait(head_rows(0, j), relay_send.at[j])
+
+        @pl.when(has_far)
+        def _():
+            wait(far_out.at[j], far_send.at[j])
+
+        @pl.when(has_behind)
+        def _():
+            wait(near_out.at[j], near_send.at[j])
+
         wait(dq.at[0:TOK, lanes(j * width, width)], dq_send.at[j])
         wait(dq.at[:, lanes(j * width, width)], dq_recv.at[j])
-        for which in range(2):
-            wait(dkv.at[which, 0:TOK, lanes(j * DIM, DIM)], dkv_send.at[which, j])
-            wait(dkv.at[which, :, lanes(j * DIM, DIM)], dkv_recv.at[which, j])
+        wait(own_out.at[j, :, 0:TOK, :], part_send.at[j])
+        wait(own_out.at[j], part_recv.at[j])
+
+        @pl.when(has_ahead)
+        def _():
+            for core in range(2):
+                wait(
+                    near_in.at[:, :, lanes(core * KVW + j * DIM, DIM)],
+                    near_recv.at[core * KVH + j],
+                )
+
+
+def finish(dq_in, near_in, own_in, dq_hbm, dk_hbm, dv_hbm, grads, sems):
+    dq_copy = pltpu.make_async_copy(dq_in, dq_hbm, sems.at[2])
+    dq_copy.start()
+    copies = [
+        pltpu.make_async_copy(grads.at[n], out, sems.at[n])
+        for n, out in enumerate((dk_hbm, dv_hbm))
+    ]
+    for n in range(2):
+        grads[n] = (own_in[n] + near_in[n].astype(jnp.float32)).astype(grads.dtype)
+        copies[n].start()
+    for copy in (dq_copy, *copies):
+        copy.wait()
 
 
 def local(chips, fsdp, queries, keys, values, grad_out, segment):
     low = jnp.bfloat16
     dma = pltpu.SemaphoreType.DMA
     anywhere = pl.BlockSpec(memory_space=pl.ANY)
-    return pl.pallas_call(
+    inside = pl.BlockSpec(memory_space=pltpu.VMEM)
+    pair = (2, TOK, 2 * KVW)
+    parts = pl.pallas_call(
         functools.partial(kernel, chips, fsdp),
         out_shape=(
-            jax.ShapeDtypeStruct(queries.shape, low),
-            jax.ShapeDtypeStruct(keys.shape, low),
-            jax.ShapeDtypeStruct(values.shape, low),
+            pltpu.VMEM((TOK, 2 * QW), low),
+            pltpu.VMEM(pair, low),
+            pltpu.VMEM(pair, jnp.float32),
         ),
         in_specs=[anywhere] * 5,
-        out_specs=(anywhere,) * 3,
+        out_specs=(inside,) * 3,
         scratch_shapes=[
             pltpu.VMEM((2, ROWS, KVW), low),
             pltpu.VMEM((CHIP, QW), low),
             pltpu.VMEM((CHIP, QW), low),
             pltpu.VMEM((6, 1, TOK), jnp.int32),
             pltpu.VMEM((2, SPAN, TOK), jnp.float32),
-            pltpu.VMEM((KVH, 2, WINDOW, DIM), jnp.float32),
-            pltpu.VMEM((KVH, 2, CHIP, DIM), low),
+            pltpu.VMEM((KVH, 2, CHIP, DIM), jnp.float32),
+            pltpu.VMEM((KVH, 2, CHIP, DIM), jnp.float32),
             pltpu.VMEM((KVH, 2, CHIP, DIM), low),
             pltpu.VMEM((KVH, 2, CHIP, DIM), low),
             pltpu.VMEM((KVH, 2, CHIP, DIM), low),
             pltpu.VMEM((CHIP, QW), low),
-            pltpu.VMEM((2, CHIP, KVW), low),
             dma((KVH,)),
             dma((KVH,)),
             dma((KVH,)),
@@ -359,18 +467,29 @@
             dma(()),
             dma(()),
             dma(()),
-            dma((KVH,)),
-            dma((KVH,)),
-            dma((KVH,)),
-            dma((KVH,)),
-            dma((KVH,)),
-            dma((KVH,)),
-            dma((2, KVH)),
-            dma((2, KVH)),
+            dma(()),
+            dma(()),
+            dma((KVH,)),
+            dma((KVH,)),
+            dma((KVH,)),
+            dma((2 * KVH,)),
+            dma((KVH,)),
+            dma((KVH,)),
+            dma((KVH,)),
+            dma((KVH,)),
+            pltpu.SemaphoreType.REGULAR,
         ],
         compiler_params=pltpu.CompilerParams(collective_id=0, has_side_effects=True),
         name="window_grads",
     )(queries, keys, values, grad_out, segment.reshape(1, TOK))
+    return pl.pallas_call(
+        finish,
+        out_shape=tuple(jax.ShapeDtypeStruct(a.shape, low) for a in (queries, keys, values)),
+        in_specs=[inside] * 3,
+        out_specs=(anywhere,) * 3,
+        scratch_shapes=[pltpu.VMEM(pair, low), dma((3,))],
+        name="window_grads_out",
+    )(*(pltpu.with_memory_space_constraint(part, pltpu.VMEM) for part in parts))
 
 
 def solution(mesh):

time: 65.7 us -> 48.3 us (0.74)
  the two profiles are of different devices: /device:TPU:1 before, /device:TPU:198 now
where the time goes in v2:
time: 48.3 us; the launch traced here: 48.1 us
  Pallas kernels  47.5 us (98%)
  between operations  0.64 us (1%)
    pallas_call x1, Pallas kernels, local(): pl.pallas_call(functools.partial(kernel, chips, fsdp), out_shape=(pltpu.V...  46.5 us
    pallas_call x1, Pallas kernels, local(): pl.pallas_call(finish, out_shape=tuple((jax.ShapeDtypeStruct(a.shape, low...  0.99 us

profile of v2, /device:TPU:198, one launch (start us, length us, event | category | flops | bytes accessed | tf_op | source)
XLA Modules:
  0.0 48.1 jit_solution(17255263235923632581)
XLA Ops:
  0.6 46.5 %window_grads.1 = (bf16[128,2048]{1,0:T(8,128)(2,1)S(1)}, bf16[2,128,1024]{2,1,0:T(8,128)(2,1)S(1)}, f32[2,128,1024]{2,1,0:T(8,128)S(1)}) custom-call(bf16[128,2048]{1,0:T(8,128)(2,1)} %q_hbm.1, bf16[128,1024]{1,0:T(8,128)(2,1)} %k_hbm.1, bf16[128,1024]{1,0:T(8,128)(2,1)} %v_hbm.1, bf16[128,2048]{1,0:T(8,128)(2,1)} %do_hbm.1, s32[1,128]{1,0:T(1,128)} %bitcast.1), custom_call_target="tpu_custom_call" | custom-call | tf_op jit(solution)/shard_map/window_grads/pallas_call | solution.py:439
  47.1 1.0 %window_grads_out.1 = (bf16[128,2048]{1,0:T(8,128)(2,1)}, bf16[128,1024]{1,0:T(8,128)(2,1)}, bf16[128,1024]{1,0:T(8,128)(2,1)}) custom-call(bf16[128,2048]{1,0:T(8,128)(2,1)S(1)} %get-tuple-element.6.dq_in, bf16[2,128,1024]{2,1,0:T(8,128)(2,1)S(1)} %get-tuple-element.7.near_in, f32[2,128,1024]{2,1,0:T(8,128)S(1)} %get-tuple-element.8.own_in), custom_call_target="tpu_custom_call" | custom-call | tf_op jit(solution)/shard_map/window_grads_out/pallas_call | solution.py:485

commit v3 on v2

--- a/solution.py
+++ b/solution.py
@@ -129,40 +129,44 @@
         signal(ready, device(ahead, 1))
 
     def send_own(j):
-        for core in range(2):
+        @pl.when(has_ahead)
+        def _():
             for which, src in ((0, k_hbm), (1, v_hbm)):
+                for core in range(2):
+                    remote(
+                        src.at[:, lanes(core * KVW + j * DIM, DIM)],
+                        kv.at[which, rows(me, CHIP), lanes(j * DIM, DIM)],
+                        own_send.at[which, j],
+                        own_recv.at[which, j],
+                        device(ahead, core),
+                    ).start()
+
+    def head_rows(which, start, j):
+        return kv.at[which, start : start + CHIP, lanes(j * DIM, DIM)]
+
+    def relay(j):
+        for which in range(2):
+            @pl.when(has_behind)
+            def _():
+                wait(head_rows(which, CHIP, j), own_recv.at[which, j])
+
+            @pl.when(has_behind & has_ahead)
+            def _():
                 remote(
-                    src.at[:, lanes(core * KVW + j * DIM, DIM)],
-                    kv.at[which, rows(me, CHIP), lanes(j * DIM, DIM)],
-                    own_send.at[j],
-                    own_recv.at[j],
-                    device(ahead, core),
+                    head_rows(which, CHIP, j),
+                    head_rows(which, 0, j),
+                    relay_send.at[which, j],
+                    relay_recv.at[which, j],
+                    device(ahead, me),
                 ).start()
-
-    def head_rows(start, j):
-        return kv.at[:, start : start + CHIP, lanes(j * DIM, DIM)]
-
-    def relay(j):
-        @pl.when(has_behind)
-        def _():
-            wait(head_rows(CHIP, j), own_recv.at[j])
-
-        @pl.when(has_behind & has_ahead)
-        def _():
-            remote(
-                head_rows(CHIP, j),
-                head_rows(0, j),
-                relay_send.at[j],
-                relay_recv.at[j],
-                device(ahead, me),
-            ).start()
 
     @pl.when(has_ahead)
     def _():
         for core in range(2):
             remote(seg_hbm, seg.at[2 + me], seg_send, seg_recv, device(ahead, core)).start()
-        send_own(0)
-        send_own(1)
+
+    send_own(0)
+    send_own(1)
 
     @pl.when(chip <= 1)
     def _():
@@ -217,7 +221,12 @@
     relay(0)
     relay(1)
 
-    @pl.when(has_ahead & has_far)
+    @pl.when(chip <= 2)
+    def _():
+        relay(2)
+        relay(3)
+
+    @pl.when(chip > 1)
     def _():
         send_own(2)
         send_own(3)
@@ -256,67 +265,83 @@
     wait(q, swap_recv.at[2])
     wait(do, swap_recv.at[3])
 
-    def unit(j, s):
-        cols = lanes(j * DIM, DIM)
-        keys = kv[0, s * TOK : s * TOK + SPAN, cols]
-        vals = kv[1, s * TOK : s * TOK + SPAN, cols]
-
-        def stacked(ref):
-            return jnp.concatenate(
-                [
-                    ref[s * TOK : (s + 1) * TOK, lanes((j * GROUP + r) * DIM, DIM)]
-                    for r in range(GROUP)
-                ],
-                axis=0,
-            )
-
-        queries = stacked(q)
-        grads = stacked(do)
+    def stacked(ref, j, s):
+        return jnp.concatenate(
+            [
+                ref[s * TOK : (s + 1) * TOK, lanes((j * GROUP + r) * DIM, DIM)]
+                for r in range(GROUP)
+            ],
+            axis=0,
+        )
+
+    def key_rows(which, j, s):
+        return kv[which, s * TOK : s * TOK + SPAN, lanes(j * DIM, DIM)]
+
+    def forward(j, s):
+        grads = stacked(do, j, s)
         seen = jnp.concatenate([mask[s]] * GROUP, axis=1)
-        t = jnp.tanh(mm(keys, queries, NT) * (SCALE / CAP))
+        t = jnp.tanh(mm(key_rows(0, j, s), stacked(q, j, s), NT) * (SCALE / CAP))
         weights = jnp.exp(CAP * t) * seen
         total = jnp.sum(weights, axis=0, keepdims=True)
         probs = weights * (1.0 / total)
         probs_low = probs.astype(jnp.bfloat16)
-        dprobs = mm(vals, grads, NT)
+        dprobs = mm(key_rows(1, j, s), grads, NT)
+        return t, probs, probs_low, dprobs, mm(probs_low, grads, NN)
+
+    def backward(j, s, t, probs, probs_low, dprobs):
         row_term = jnp.sum(probs_low.astype(jnp.float32) * dprobs, axis=0, keepdims=True)
         dscore = probs * (dprobs - row_term) * ((1.0 - t * t) * SCALE)
         dscore_low = dscore.astype(jnp.bfloat16)
-        grad_k = mm(dscore_low, queries, NN)
-        grad_v = mm(probs_low, grads, NN)
-        grad_q = mm(keys, dscore_low, TN).T
+        grad_q = mm(key_rows(0, j, s), dscore_low, TN).T
         for r in range(GROUP):
             dq[s * TOK : (s + 1) * TOK, lanes((j * GROUP + r) * DIM, DIM)] = grad_q[
                 r * TOK : (r + 1) * TOK
             ].astype(jnp.bfloat16)
-        return grad_k, grad_v
-
-    def far_copy(j):
+        return mm(dscore_low, stacked(q, j, s), NN)
+
+    def far_copy(which, j):
         return remote(
-            far_out.at[j], far_in.at[j], far_send.at[j], far_recv.at[j], device(behind, me)
+            far_out.at[j, which],
+            far_in.at[j, which],
+            far_send.at[which, j],
+            far_recv.at[which, j],
+            device(behind, me),
         )
 
-    def send_near(j):
+    def hand_out(which, j, low, high):
+        far_out[j, which, 0:TOK, :] = low[0:TOK].astype(jnp.bfloat16)
+        far_out[j, which, TOK:CHIP, :] = (low[TOK:CHIP] + high[0:TOK]).astype(jnp.bfloat16)
+
+        @pl.when(has_far)
+        def _():
+            far_copy(which, j).start()
+
+        part[j, which] = low[CHIP:WINDOW] + high[TOK : WINDOW - TOK]
+        own_out[j, which, 0:TOK, :] = low[WINDOW:SPAN] + high[WINDOW - TOK : WINDOW]
+        own_out[j, which, TOK:CHIP, :] = high[WINDOW:SPAN]
+
+    def send_near(which, j):
         for core in range(2):
             remote(
-                near_out.at[j, :, core * TOK : (core + 1) * TOK, :],
-                near_in.at[:, :, lanes(me * KVW + j * DIM, DIM)],
-                near_send.at[j],
-                near_recv.at[me * KVH + j],
+                near_out.at[j, which, core * TOK : (core + 1) * TOK, :],
+                near_in.at[which, :, lanes(me * KVW + j * DIM, DIM)],
+                near_send.at[which, j],
+                near_recv.at[which, me * KVH + j],
                 device(behind, core),
             ).start()
 
     def pass_on(j):
         @pl.when(has_behind)
         def _():
-            @pl.when(has_ahead)
-            def _():
-                wait(far_in.at[j], far_recv.at[j])
-
-            near_out[j] = (part[j] + far_in[j].astype(jnp.float32)).astype(
-                jnp.bfloat16
-            )
-            send_near(j)
+            for which in (1, 0):
+                @pl.when(has_ahead)
+                def _():
+                    wait(far_in.at[j, which], far_recv.at[which, j])
+
+                near_out[j, which] = (
+                    part[j, which] + far_in[j, which].astype(jnp.float32)
+                ).astype(jnp.bfloat16)
+                send_near(which, j)
 
     def swap(j):
         width = GROUP * DIM
@@ -342,34 +367,36 @@
     def _(j):
         @pl.when(has_far)
         def _():
-            wait(head_rows(0, j), relay_recv.at[j])
-
-        first = unit(j, 0)
-        second = unit(j, 1)
-        for which in range(2):
-            low, high = first[which], second[which]
-            far_out[j, which, 0:TOK, :] = low[0:TOK].astype(jnp.bfloat16)
-            far_out[j, which, TOK:CHIP, :] = (low[TOK:CHIP] + high[0:TOK]).astype(jnp.bfloat16)
-            part[j, which] = low[CHIP:WINDOW] + high[TOK : WINDOW - TOK]
-            own_out[j, which, 0:TOK, :] = low[WINDOW:SPAN] + high[WINDOW - TOK : WINDOW]
-            own_out[j, which, TOK:CHIP, :] = high[WINDOW:SPAN]
-
-        @pl.when(has_far)
-        def _():
-            far_copy(j).start()
+            for which in range(2):
+                wait(head_rows(which, 0, j), relay_recv.at[which, j])
+
+        *first, low = forward(j, 0)
+        *second, high = forward(j, 1)
+        hand_out(1, j, low, high)
+        hand_out(0, j, backward(j, 0, *first), backward(j, 1, *second))
 
         swap(j)
 
         @pl.when(j == 1)
         def _():
             for n in range(2):
-                relay(n + 2)
-                pass_on(n)
+                @pl.when(chip > 2)
+                def _():
+                    relay(n + 2)
+
+                @pl.when(chip != 2)
+                def _():
+                    pass_on(n)
 
         @pl.when(j == KVH - 1)
         def _():
-            pass_on(KVH - 2)
-            pass_on(KVH - 1)
+            @pl.when(chip == 2)
+            def _():
+                pass_on(0)
+                pass_on(1)
+
+            pass_on(2)
+            pass_on(3)
 
     @pl.when(has_ahead)
     def _():
@@ -386,21 +413,22 @@
     @pl.loop(0, KVH)
     def _(j):
         width = GROUP * DIM
-        @pl.when(has_ahead)
-        def _():
-            wait(head_rows(CHIP, j), own_send.at[j])
-
-        @pl.when(has_behind & has_ahead)
-        def _():
-            wait(head_rows(0, j), relay_send.at[j])
-
-        @pl.when(has_far)
-        def _():
-            wait(far_out.at[j], far_send.at[j])
-
-        @pl.when(has_behind)
-        def _():
-            wait(near_out.at[j], near_send.at[j])
+        for which in range(2):
+            @pl.when(has_ahead)
+            def _():
+                wait(head_rows(which, CHIP, j), own_send.at[which, j])
+
+            @pl.when(has_behind & has_ahead)
+            def _():
+                wait(head_rows(which, 0, j), relay_send.at[which, j])
+
+            @pl.when(has_far)
+            def _():
+                wait(far_out.at[j, which], far_send.at[which, j])
+
+            @pl.when(has_behind)
+            def _():
+                wait(near_out.at[j, which], near_send.at[which, j])
 
         wait(dq.at[0:TOK, lanes(j * width, width)], dq_send.at[j])
         wait(dq.at[:, lanes(j * width, width)], dq_recv.at[j])
@@ -409,11 +437,12 @@
 
         @pl.when(has_ahead)
         def _():
-            for core in range(2):
-                wait(
-                    near_in.at[:, :, lanes(core * KVW + j * DIM, DIM)],
-                    near_recv.at[core * KVH + j],
-                )
+            for which in range(2):
+                for core in range(2):
+                    wait(
+                        near_in.at[which, :, lanes(core * KVW + j * DIM, DIM)],
+                        near_recv.at[which, core * KVH + j],
+                    )
 
 
 def finish(dq_in, near_in, own_in, dq_hbm, dk_hbm, dv_hbm, grads, sems):
@@ -457,10 +486,10 @@
             pltpu.VMEM((KVH, 2, CHIP, DIM), low),
             pltpu.VMEM((KVH, 2, CHIP, DIM), low),
             pltpu.VMEM((CHIP, QW), low),
-            dma((KVH,)),
-            dma((KVH,)),
-            dma((KVH,)),
-            dma((KVH,)),
+            dma((2, KVH)),
+            dma((2, KVH)),
+            dma((2, KVH)),
+            dma((2, KVH)),
             dma((4,)),
             dma((4,)),
             dma(()),
@@ -469,10 +498,10 @@
             dma(()),
             dma(()),
             dma(()),
-            dma((KVH,)),
-            dma((KVH,)),
-            dma((KVH,)),
-            dma((2 * KVH,)),
+            dma((2, KVH)),
+            dma((2, KVH)),
+            dma((2, KVH)),
+            dma((2, 2 * KVH)),
             dma((KVH,)),
             dma((KVH,)),
             dma((KVH,)),

time: 48.3 us -> 46.4 us (0.961)
  the two profiles are of different devices: /device:TPU:198 before, /device:TPU:9 now
where the time goes in v3:
time: 46.4 us; the launch traced here: 46.3 us
  Pallas kernels  45.7 us (98%)
  between operations  0.64 us (1%)
    pallas_call x1, Pallas kernels, local(): pl.pallas_call(functools.partial(kernel, chips, fsdp), out_shape=(pltpu.V...  44.7 us
    pallas_call x1, Pallas kernels, local(): pl.pallas_call(finish, out_shape=tuple((jax.ShapeDtypeStruct(a.shape, low...  0.99 us

profile of v3, /device:TPU:9, one launch (start us, length us, event | category | flops | bytes accessed | tf_op | source)
XLA Modules:
  0.0 46.3 jit_solution(7598769195531857231)
XLA Ops:
  0.6 44.7 %window_grads.1 = (bf16[128,2048]{1,0:T(8,128)(2,1)S(1)}, bf16[2,128,1024]{2,1,0:T(8,128)(2,1)S(1)}, f32[2,128,1024]{2,1,0:T(8,128)S(1)}) custom-call(bf16[128,2048]{1,0:T(8,128)(2,1)} %q_hbm.1, bf16[128,1024]{1,0:T(8,128)(2,1)} %k_hbm.1, bf16[128,1024]{1,0:T(8,128)(2,1)} %v_hbm.1, bf16[128,2048]{1,0:T(8,128)(2,1)} %do_hbm.1, s32[1,128]{1,0:T(1,128)} %bitcast.1), custom_call_target="tpu_custom_call" | custom-call | tf_op jit(solution)/shard_map/window_grads/pallas_call | solution.py:468
  45.3 1.0 %window_grads_out.1 = (bf16[128,2048]{1,0:T(8,128)(2,1)}, bf16[128,1024]{1,0:T(8,128)(2,1)}, bf16[128,1024]{1,0:T(8,128)(2,1)}) custom-call(bf16[128,2048]{1,0:T(8,128)(2,1)S(1)} %get-tuple-element.6.dq_in, bf16[2,128,1024]{2,1,0:T(8,128)(2,1)S(1)} %get-tuple-element.7.near_in, f32[2,128,1024]{2,1,0:T(8,128)S(1)} %get-tuple-element.8.own_in), custom_call_target="tpu_custom_call" | custom-call | tf_op jit(solution)/shard_map/window_grads_out/pallas_call | solution.py:514

commit v4 on v3

--- a/solution.py
+++ b/solution.py
@@ -74,18 +74,26 @@
     part_recv,
     ready,
 ):
-    index = lax.axis_index("ctx") * fsdp + lax.axis_index("fsdp")
-    chip = index // 2
-    me = index % 2
+    row, column = lax.axis_index("ctx"), lax.axis_index("fsdp")
+    me = column % 2
     other = 1 - me
-
-    def device(which_chip, core):
-        at = which_chip * 2 + core
-        return (at // fsdp, at % fsdp)
-
-    ahead = (chip + 1) % chips
-    behind = (chip + chips - 1) % chips
-    partner = device(chip, other)
+    start = column - me
+    row_chips = fsdp // 2
+    chip = row * row_chips + start // 2
+    partner = (row, start + other)
+    rows_all = chips // row_chips
+    turns, turned = start == fsdp - 2, start == 0
+    ahead = (
+        jnp.where(turns, jnp.where(row == rows_all - 1, 0, row + 1), row),
+        jnp.where(turns, 0, start + 2),
+    )
+    behind = (
+        jnp.where(turned, jnp.where(row == 0, rows_all - 1, row - 1), row),
+        jnp.where(turned, fsdp - 2, start - 2),
+    )
+
+    def device(at, core):
+        return (at[0], at[1] + core)
 
     def remote(src, dst, send, recv, to):
         return pltpu.make_async_remote_copy(
@@ -114,13 +122,13 @@
         pl.semaphore_signal(sem, inc=1, device_id=to, device_id_type=pl.DeviceIdType.MESH)
 
     barrier = pltpu.get_barrier_semaphore()
-    signal(barrier, partner)
 
     @pl.when(has_behind)
     def _():
         signal(barrier, device(behind, 0))
         signal(barrier, device(behind, 1))
 
+    signal(barrier, partner)
     pl.semaphore_wait(barrier, 1 + 2 * jnp.where(has_ahead, 1, 0))
 
     @pl.when(has_ahead)
@@ -274,30 +282,19 @@
             axis=0,
         )
 
-    def key_rows(which, j, s):
-        return kv[which, s * TOK : s * TOK + SPAN, lanes(j * DIM, DIM)]
-
-    def forward(j, s):
-        grads = stacked(do, j, s)
-        seen = jnp.concatenate([mask[s]] * GROUP, axis=1)
-        t = jnp.tanh(mm(key_rows(0, j, s), stacked(q, j, s), NT) * (SCALE / CAP))
-        weights = jnp.exp(CAP * t) * seen
-        total = jnp.sum(weights, axis=0, keepdims=True)
-        probs = weights * (1.0 / total)
-        probs_low = probs.astype(jnp.bfloat16)
-        dprobs = mm(key_rows(1, j, s), grads, NT)
-        return t, probs, probs_low, dprobs, mm(probs_low, grads, NN)
-
-    def backward(j, s, t, probs, probs_low, dprobs):
-        row_term = jnp.sum(probs_low.astype(jnp.float32) * dprobs, axis=0, keepdims=True)
+    def scores(j, s, queries, grads, low, high):
+        keys = kv[0, low:high, lanes(j * DIM, DIM)]
+        vals = kv[1, low:high, lanes(j * DIM, DIM)]
+        seen = jnp.concatenate([mask[s, low - s * TOK : high - s * TOK]] * GROUP, axis=1)
+        t = jnp.tanh(mm(keys, queries, NT) * (SCALE / CAP))
+        return t, jnp.exp(CAP * t) * seen, mm(vals, grads, NT)
+
+    def column_sum(a):
+        return jnp.sum(a, axis=0, keepdims=True)
+
+    def score_grads(t, probs, dprobs, row_term):
         dscore = probs * (dprobs - row_term) * ((1.0 - t * t) * SCALE)
-        dscore_low = dscore.astype(jnp.bfloat16)
-        grad_q = mm(key_rows(0, j, s), dscore_low, TN).T
-        for r in range(GROUP):
-            dq[s * TOK : (s + 1) * TOK, lanes((j * GROUP + r) * DIM, DIM)] = grad_q[
-                r * TOK : (r + 1) * TOK
-            ].astype(jnp.bfloat16)
-        return mm(dscore_low, stacked(q, j, s), NN)
+        return dscore.astype(jnp.bfloat16)
 
     def far_copy(which, j):
         return remote(
@@ -308,17 +305,18 @@
             device(behind, me),
         )
 
-    def hand_out(which, j, low, high):
+    def far_out_of(which, j, low, high):
         far_out[j, which, 0:TOK, :] = low[0:TOK].astype(jnp.bfloat16)
-        far_out[j, which, TOK:CHIP, :] = (low[TOK:CHIP] + high[0:TOK]).astype(jnp.bfloat16)
+        far_out[j, which, TOK:CHIP, :] = (low[TOK:CHIP] + high).astype(jnp.bfloat16)
 
         @pl.when(has_far)
         def _():
             far_copy(which, j).start()
 
-        part[j, which] = low[CHIP:WINDOW] + high[TOK : WINDOW - TOK]
-        own_out[j, which, 0:TOK, :] = low[WINDOW:SPAN] + high[WINDOW - TOK : WINDOW]
-        own_out[j, which, TOK:CHIP, :] = high[WINDOW:SPAN]
+    def rest_of(which, j, low, high):
+        part[j, which] = low[0:CHIP] + high[0:CHIP]
+        own_out[j, which, 0:TOK, :] = low[CHIP : CHIP + TOK] + high[CHIP : CHIP + TOK]
+        own_out[j, which, TOK:CHIP, :] = high[CHIP + TOK : WINDOW]
 
     def send_near(which, j):
         for core in range(2):
@@ -365,15 +363,46 @@
 
     @pl.loop(0, KVH)
     def _(j):
+        queries = [stacked(q, j, s) for s in range(2)]
+        grads = [stacked(do, j, s) for s in range(2)]
+
+        near = [scores(j, s, queries[s], grads[s], CHIP, s * TOK + SPAN) for s in range(2)]
+
         @pl.when(has_far)
         def _():
             for which in range(2):
                 wait(head_rows(which, 0, j), relay_recv.at[which, j])
 
-        *first, low = forward(j, 0)
-        *second, high = forward(j, 1)
-        hand_out(1, j, low, high)
-        hand_out(0, j, backward(j, 0, *first), backward(j, 1, *second))
+        far = [scores(j, s, queries[s], grads[s], s * TOK, CHIP) for s in range(2)]
+        probs = []
+        for s in range(2):
+            inverse = 1.0 / (column_sum(far[s][1]) + column_sum(near[s][1]))
+            probs.append((far[s][1] * inverse, near[s][1] * inverse))
+        low = [[p.astype(jnp.bfloat16) for p in pair] for pair in probs]
+        far_out_of(1, j, *(mm(low[s][0], grads[s], NN) for s in range(2)))
+
+        far_low, row_terms = [], []
+        for s in range(2):
+            row_terms.append(
+                column_sum(low[s][0].astype(jnp.float32) * far[s][2])
+                + column_sum(low[s][1].astype(jnp.float32) * near[s][2])
+            )
+            far_low.append(score_grads(far[s][0], probs[s][0], far[s][2], row_terms[s]))
+        far_out_of(0, j, *(mm(far_low[s], queries[s], NN) for s in range(2)))
+
+        near_low = [
+            score_grads(near[s][0], probs[s][1], near[s][2], row_terms[s]) for s in range(2)
+        ]
+        rest_of(1, j, *(mm(low[s][1], grads[s], NN) for s in range(2)))
+        rest_of(0, j, *(mm(near_low[s], queries[s], NN) for s in range(2)))
+        for s in range(2):
+            keys = kv[0, s * TOK : s * TOK + SPAN, lanes(j * DIM, DIM)]
+            both = jnp.concatenate([far_low[s], near_low[s]], axis=0)
+            grad_q = mm(keys, both, TN).T
+            for r in range(GROUP):
+                dq[s * TOK : (s + 1) * TOK, lanes((j * GROUP + r) * DIM, DIM)] = grad_q[
+                    r * TOK : (r + 1) * TOK
+                ].astype(jnp.bfloat16)
 
         swap(j)
 

time: 46.4 us -> 46.1 us (level)
  no operation moved by 1% of the time
where the time goes in v4:
time: 46.1 us; the launch traced here: 46 us
  Pallas kernels  45.3 us (98%)
  between operations  0.64 us (1%)
    pallas_call x1, Pallas kernels, local(): pl.pallas_call(functools.partial(kernel, chips, fsdp), out_shape=(pltpu.V...  44.3 us
    pallas_call x1, Pallas kernels, local(): pl.pallas_call(finish, out_shape=tuple((jax.ShapeDtypeStruct(a.shape, low...  0.99 us

profile of v4, /device:TPU:9, one launch (start us, length us, event | category | flops | bytes accessed | tf_op | source)
XLA Modules:
  0.0 46.0 jit_solution(12028794946275965498)
XLA Ops:
  0.6 44.3 %window_grads.1 = (bf16[128,2048]{1,0:T(8,128)(2,1)S(1)}, bf16[2,128,1024]{2,1,0:T(8,128)(2,1)S(1)}, f32[2,128,1024]{2,1,0:T(8,128)S(1)}) custom-call(bf16[128,2048]{1,0:T(8,128)(2,1)} %q_hbm.1, bf16[128,1024]{1,0:T(8,128)(2,1)} %k_hbm.1, bf16[128,1024]{1,0:T(8,128)(2,1)} %v_hbm.1, bf16[128,2048]{1,0:T(8,128)(2,1)} %do_hbm.1, s32[1,128]{1,0:T(1,128)} %bitcast.1), custom_call_target="tpu_custom_call" | custom-call | tf_op jit(solution)/shard_map/window_grads/pallas_call | solution.py:497
  45.0 1.0 %window_grads_out.1 = (bf16[128,2048]{1,0:T(8,128)(2,1)}, bf16[128,1024]{1,0:T(8,128)(2,1)}, bf16[128,1024]{1,0:T(8,128)(2,1)}) custom-call(bf16[128,2048]{1,0:T(8,128)(2,1)S(1)} %get-tuple-element.6.dq_in, bf16[2,128,1024]{2,1,0:T(8,128)(2,1)S(1)} %get-tuple-element.7.near_in, f32[2,128,1024]{2,1,0:T(8,128)S(1)} %get-tuple-element.8.own_in), custom_call_target="tpu_custom_call" | custom-call | tf_op jit(solution)/shard_map/window_grads_out/pallas_call | solution.py:543

commit v5 on v4

--- a/solution.py
+++ b/solution.py
@@ -229,15 +229,15 @@
     relay(0)
     relay(1)
 
+    @pl.when(chip > 1)
+    def _():
+        send_own(2)
+        send_own(3)
+
     @pl.when(chip <= 2)
     def _():
         relay(2)
         relay(3)
-
-    @pl.when(chip > 1)
-    def _():
-        send_own(2)
-        send_own(3)
 
     wait(seg.at[4:6], seg_swap_recv)
 
@@ -282,12 +282,14 @@
             axis=0,
         )
 
-    def scores(j, s, queries, grads, low, high):
+    def scores(j, s, queries, low, high):
         keys = kv[0, low:high, lanes(j * DIM, DIM)]
-        vals = kv[1, low:high, lanes(j * DIM, DIM)]
         seen = jnp.concatenate([mask[s, low - s * TOK : high - s * TOK]] * GROUP, axis=1)
         t = jnp.tanh(mm(keys, queries, NT) * (SCALE / CAP))
-        return t, jnp.exp(CAP * t) * seen, mm(vals, grads, NT)
+        return t, jnp.exp(CAP * t) * seen
+
+    def prob_grads(j, grads, low, high):
+        return mm(kv[1, low:high, lanes(j * DIM, DIM)], grads, NT)
 
     def column_sum(a):
         return jnp.sum(a, axis=0, keepdims=True)
@@ -366,14 +368,14 @@
         queries = [stacked(q, j, s) for s in range(2)]
         grads = [stacked(do, j, s) for s in range(2)]
 
-        near = [scores(j, s, queries[s], grads[s], CHIP, s * TOK + SPAN) for s in range(2)]
+        near = [scores(j, s, queries[s], CHIP, s * TOK + SPAN) for s in range(2)]
+        near_dprobs = [prob_grads(j, grads[s], CHIP, s * TOK + SPAN) for s in range(2)]
 
         @pl.when(has_far)
         def _():
-            for which in range(2):
-                wait(head_rows(which, 0, j), relay_recv.at[which, j])
-
-        far = [scores(j, s, queries[s], grads[s], s * TOK, CHIP) for s in range(2)]
+            wait(head_rows(0, 0, j), relay_recv.at[0, j])
+
+        far = [scores(j, s, queries[s], s * TOK, CHIP) for s in range(2)]
         probs = []
         for s in range(2):
             inverse = 1.0 / (column_sum(far[s][1]) + column_sum(near[s][1]))
@@ -381,17 +383,25 @@
         low = [[p.astype(jnp.bfloat16) for p in pair] for pair in probs]
         far_out_of(1, j, *(mm(low[s][0], grads[s], NN) for s in range(2)))
 
+        near_terms = [
+            column_sum(low[s][1].astype(jnp.float32) * near_dprobs[s]) for s in range(2)
+        ]
+
+        @pl.when(has_far)
+        def _():
+            wait(head_rows(1, 0, j), relay_recv.at[1, j])
+
         far_low, row_terms = [], []
         for s in range(2):
+            dprobs = prob_grads(j, grads[s], s * TOK, CHIP)
             row_terms.append(
-                column_sum(low[s][0].astype(jnp.float32) * far[s][2])
-                + column_sum(low[s][1].astype(jnp.float32) * near[s][2])
+                column_sum(low[s][0].astype(jnp.float32) * dprobs) + near_terms[s]
             )
-            far_low.append(score_grads(far[s][0], probs[s][0], far[s][2], row_terms[s]))
+            far_low.append(score_grads(far[s][0], probs[s][0], dprobs, row_terms[s]))
         far_out_of(0, j, *(mm(far_low[s], queries[s], NN) for s in range(2)))
 
         near_low = [
-            score_grads(near[s][0], probs[s][1], near[s][2], row_terms[s]) for s in range(2)
+            score_grads(near[s][0], probs[s][1], near_dprobs[s], row_terms[s]) for s in range(2)
         ]
         rest_of(1, j, *(mm(low[s][1], grads[s], NN) for s in range(2)))
         rest_of(0, j, *(mm(near_low[s], queries[s], NN) for s in range(2)))

time: 46.1 us -> 45.2 us (0.980)
  the two profiles are of different devices: /device:TPU:9 before, /device:TPU:571 now
where the time goes in v5:
time: 45.2 us; the launch traced here: 45.1 us
  Pallas kernels  44.4 us (98%)
  between operations  0.64 us (1%)
    pallas_call x1, Pallas kernels, local(): pl.pallas_call(functools.partial(kernel, chips, fsdp), out_shape=(pltpu.V...  43.4 us
    pallas_call x1, Pallas kernels, local(): pl.pallas_call(finish, out_shape=tuple((jax.ShapeDtypeStruct(a.shape, low...  0.99 us

profile of v5, /device:TPU:571, one launch (start us, length us, event | category | flops | bytes accessed | tf_op | source)
XLA Modules:
  0.0 45.1 jit_solution(16117609462383650282)
XLA Ops:
  0.6 43.4 %window_grads.1 = (bf16[128,2048]{1,0:T(8,128)(2,1)S(1)}, bf16[2,128,1024]{2,1,0:T(8,128)(2,1)S(1)}, f32[2,128,1024]{2,1,0:T(8,128)S(1)}) custom-call(bf16[128,2048]{1,0:T(8,128)(2,1)} %q_hbm.1, bf16[128,1024]{1,0:T(8,128)(2,1)} %k_hbm.1, bf16[128,1024]{1,0:T(8,128)(2,1)} %v_hbm.1, bf16[128,2048]{1,0:T(8,128)(2,1)} %do_hbm.1, s32[1,128]{1,0:T(1,128)} %bitcast.1), custom_call_target="tpu_custom_call" | custom-call | tf_op jit(solution)/shard_map/window_grads/pallas_call | solution.py:507
  44.1 1.0 %window_grads_out.1 = (bf16[128,2048]{1,0:T(8,128)(2,1)}, bf16[128,1024]{1,0:T(8,128)(2,1)}, bf16[128,1024]{1,0:T(8,128)(2,1)}) custom-call(bf16[128,2048]{1,0:T(8,128)(2,1)S(1)} %get-tuple-element.6.dq_in, bf16[2,128,1024]{2,1,0:T(8,128)(2,1)S(1)} %get-tuple-element.7.near_in, f32[2,128,1024]{2,1,0:T(8,128)S(1)} %get-tuple-element.8.own_in), custom_call_target="tpu_custom_call" | custom-call | tf_op jit(solution)/shard_map/window_grads_out/pallas_call | solution.py:553

commit v6 on v5

--- a/solution.py
+++ b/solution.py
@@ -152,21 +152,24 @@
     def head_rows(which, start, j):
         return kv.at[which, start : start + CHIP, lanes(j * DIM, DIM)]
 
+    def relay_one(which, j):
+        @pl.when(has_behind)
+        def _():
+            wait(head_rows(which, CHIP, j), own_recv.at[which, j])
+
+        @pl.when(has_behind & has_ahead)
+        def _():
+            remote(
+                head_rows(which, CHIP, j),
+                head_rows(which, 0, j),
+                relay_send.at[which, j],
+                relay_recv.at[which, j],
+                device(ahead, me),
+            ).start()
+
     def relay(j):
         for which in range(2):
-            @pl.when(has_behind)
-            def _():
-                wait(head_rows(which, CHIP, j), own_recv.at[which, j])
-
-            @pl.when(has_behind & has_ahead)
-            def _():
-                remote(
-                    head_rows(which, CHIP, j),
-                    head_rows(which, 0, j),
-                    relay_send.at[which, j],
-                    relay_recv.at[which, j],
-                    device(ahead, me),
-                ).start()
+            relay_one(which, j)
 
     @pl.when(has_ahead)
     def _():
@@ -330,18 +333,21 @@
                 device(behind, core),
             ).start()
 
+    def pass_one(which, j):
+        @pl.when(has_behind)
+        def _():
+            @pl.when(has_ahead)
+            def _():
+                wait(far_in.at[j, which], far_recv.at[which, j])
+
+            near_out[j, which] = (
+                part[j, which] + far_in[j, which].astype(jnp.float32)
+            ).astype(jnp.bfloat16)
+            send_near(which, j)
+
     def pass_on(j):
-        @pl.when(has_behind)
-        def _():
-            for which in (1, 0):
-                @pl.when(has_ahead)
-                def _():
-                    wait(far_in.at[j, which], far_recv.at[which, j])
-
-                near_out[j, which] = (
-                    part[j, which] + far_in[j, which].astype(jnp.float32)
-                ).astype(jnp.bfloat16)
-                send_near(which, j)
+        for which in (1, 0):
+            pass_one(which, j)
 
     def swap(j):
         width = GROUP * DIM
@@ -416,18 +422,18 @@
 
         swap(j)
 
-        @pl.when(j == 1)
+        @pl.when(chip <= 1)
+        def _():
+            pass_on(j)
+
+        @pl.when((j == 1) & (chip > 2))
         def _():
             for n in range(2):
-                @pl.when(chip > 2)
-                def _():
-                    relay(n + 2)
-
-                @pl.when(chip != 2)
-                def _():
-                    pass_on(n)
-
-        @pl.when(j == KVH - 1)
+                for which in range(2):
+                    relay_one(which, n + 2)
+                    pass_one(1 - which, n)
+
+        @pl.when((j == KVH - 1) & (chip > 1))
         def _():
             @pl.when(chip == 2)
             def _():

time: 45.2 us -> 45.1 us (level)
  the two profiles are of different devices: /device:TPU:571 before, /device:TPU:9 now
where the time goes in v6:
time: 45.1 us; the launch traced here: 45 us
  Pallas kernels  44.4 us (98%)
  between operations  0.64 us (1%)
    pallas_call x1, Pallas kernels, local(): pl.pallas_call(functools.partial(kernel, chips, fsdp), out_shape=(pltpu.V...  43.4 us
    pallas_call x1, Pallas kernels, local(): pl.pallas_call(finish, out_shape=tuple((jax.ShapeDtypeStruct(a.shape, low...  0.99 us

profile of v6, /device:TPU:9, one launch (start us, length us, event | category | flops | bytes accessed | tf_op | source)
XLA Modules:
  0.0 45.0 jit_solution(17037771894971486765)
XLA Ops:
  0.6 43.4 %window_grads.1 = (bf16[128,2048]{1,0:T(8,128)(2,1)S(1)}, bf16[2,128,1024]{2,1,0:T(8,128)(2,1)S(1)}, f32[2,128,1024]{2,1,0:T(8,128)S(1)}) custom-call(bf16[128,2048]{1,0:T(8,128)(2,1)} %q_hbm.1, bf16[128,1024]{1,0:T(8,128)(2,1)} %k_hbm.1, bf16[128,1024]{1,0:T(8,128)(2,1)} %v_hbm.1, bf16[128,2048]{1,0:T(8,128)(2,1)} %do_hbm.1, s32[1,128]{1,0:T(1,128)} %bitcast.1), custom_call_target="tpu_custom_call" | custom-call | tf_op jit(solution)/shard_map/window_grads/pallas_call | solution.py:513
  44.0 1.0 %window_grads_out.1 = (bf16[128,2048]{1,0:T(8,128)(2,1)}, bf16[128,1024]{1,0:T(8,128)(2,1)}, bf16[128,1024]{1,0:T(8,128)(2,1)}) custom-call(bf16[128,2048]{1,0:T(8,128)(2,1)S(1)} %get-tuple-element.6.dq_in, bf16[2,128,1024]{2,1,0:T(8,128)(2,1)S(1)} %get-tuple-element.7.near_in, f32[2,128,1024]{2,1,0:T(8,128)S(1)} %get-tuple-element.8.own_in), custom_call_target="tpu_custom_call" | custom-call | tf_op jit(solution)/shard_map/window_grads_out/pallas_call | solution.py:559

commit v7 on v6

--- a/solution.py
+++ b/solution.py
@@ -491,15 +491,20 @@
 
 
 def finish(dq_in, near_in, own_in, dq_hbm, dk_hbm, dv_hbm, grads, sems):
-    dq_copy = pltpu.make_async_copy(dq_in, dq_hbm, sems.at[2])
+    dq_copy = pltpu.make_async_copy(dq_in, dq_hbm, sems.at[4])
     dq_copy.start()
-    copies = [
-        pltpu.make_async_copy(grads.at[n], out, sems.at[n])
-        for n, out in enumerate((dk_hbm, dv_hbm))
-    ]
-    for n in range(2):
-        grads[n] = (own_in[n] + near_in[n].astype(jnp.float32)).astype(grads.dtype)
-        copies[n].start()
+    copies = []
+    for n, out in enumerate((dk_hbm, dv_hbm)):
+        for half in range(2):
+            at = pl.ds(half * TOK // 2, TOK // 2)
+            grads[n, at, :] = (
+                own_in[n, at, :] + near_in[n, at, :].astype(jnp.float32)
+            ).astype(grads.dtype)
+            copy = pltpu.make_async_copy(
+                grads.at[n, at, :], out.at[at, :], sems.at[2 * n + half]
+            )
+            copy.start()
+            copies.append(copy)
     for copy in (dq_copy, *copies):
         copy.wait()
 
@@ -561,7 +566,7 @@
         out_shape=tuple(jax.ShapeDtypeStruct(a.shape, low) for a in (queries, keys, values)),
         in_specs=[inside] * 3,
         out_specs=(anywhere,) * 3,
-        scratch_shapes=[pltpu.VMEM(pair, low), dma((3,))],
+        scratch_shapes=[pltpu.VMEM(pair, low), dma((5,))],
         name="window_grads_out",
     )(*(pltpu.with_memory_space_constraint(part, pltpu.VMEM) for part in parts))
 

time: 45.1 us -> 45.2 us (level)
  no operation moved by 1% of the time
where the time goes in v7:
time: 45.2 us; the launch traced here: 45 us
  Pallas kernels  44.4 us (98%)
  between operations  0.64 us (1%)
    pallas_call x1, Pallas kernels, local(): pl.pallas_call(functools.partial(kernel, chips, fsdp), out_shape=(pltpu.V...  43.4 us
    pallas_call x1, Pallas kernels, local(): pl.pallas_call(finish, out_shape=tuple((jax.ShapeDtypeStruct(a.shape, low...  1 us

profile of v7, /device:TPU:9, one launch (start us, length us, event | category | flops | bytes accessed | tf_op | source)
XLA Modules:
  0.0 45.0 jit_solution(621635676611876892)
XLA Ops:
  0.6 43.4 %window_grads.1 = (bf16[128,2048]{1,0:T(8,128)(2,1)S(1)}, bf16[2,128,1024]{2,1,0:T(8,128)(2,1)S(1)}, f32[2,128,1024]{2,1,0:T(8,128)S(1)}) custom-call(bf16[128,2048]{1,0:T(8,128)(2,1)} %q_hbm.1, bf16[128,1024]{1,0:T(8,128)(2,1)} %k_hbm.1, bf16[128,1024]{1,0:T(8,128)(2,1)} %v_hbm.1, bf16[128,2048]{1,0:T(8,128)(2,1)} %do_hbm.1, s32[1,128]{1,0:T(1,128)} %bitcast.1), custom_call_target="tpu_custom_call" | custom-call | tf_op jit(solution)/shard_map/window_grads/pallas_call | solution.py:518
  44.0 1.0 %window_grads_out.1 = (bf16[128,2048]{1,0:T(8,128)(2,1)}, bf16[128,1024]{1,0:T(8,128)(2,1)}, bf16[128,1024]{1,0:T(8,128)(2,1)}) custom-call(bf16[128,2048]{1,0:T(8,128)(2,1)S(1)} %get-tuple-element.6.dq_in, bf16[2,128,1024]{2,1,0:T(8,128)(2,1)S(1)} %get-tuple-element.7.near_in, f32[2,128,1024]{2,1,0:T(8,128)S(1)} %get-tuple-element.8.own_in), custom_call_target="tpu_custom_call" | custom-call | tf_op jit(solution)/shard_map/window_grads_out/pallas_call | solution.py:564
